TPU v7x, 128 devices: a whole 4x4x4 slice. The times are simulated.
128 devices in a mesh: ctx: 16 (over x, z), head: 8 (over y, core).
Axes of the slice: x: 4, y: 4, z: 4, core: 2. Of those that a mesh axis runs over, the one named last changes fastest.
Arguments:
- xbc: bfloat16 [16384, 18432], P(('ctx', 'head')), may hold values from -6 to 6
- dt_raw: bfloat16 [16384, 256], P(('ctx', 'head')), may hold values from -8 to 0
- decay_rate: float32 [256], P('head'), may hold values from 0.001 to 0.3
- skip: float32 [256], P('head'), may hold values from 0.5 to 1.5
- conv_w: bfloat16 [4, 18432], P(None, 'head'), may hold values from -3 to 3
- conv_b: bfloat16 [18432], P('head'), may hold values from -3 to 3
- gain: bfloat16 [16384], P('head'), may hold values from 0.5 to 1.5
- starts: int32 [16], replicated, may hold values from 0 to 1024, as said below
- assign: int32 [4], replicated, may hold values from 0 to 15, as said below
Outputs:
- mixed: bfloat16 [16384, 16384], P(('ctx', 'head'))
- decode_states: float32 [16, 256, 64, 128], P('ctx', 'head')
- decode_tails: bfloat16 [16, 3, 18432], P('ctx', None, 'head')
Inputs may be any that keep to these rules, and one draw needn't show every extreme that they name: starts[0] = 0; exactly 4 entries are below 1024, each a multiple of 512; the others equal 1024. `assign`: the 4 entries are distinct.
All inputs are finite; a program needn't handle non-finite values.
Results may differ from a plain program's by a relative error of at most 0.0036.
Values may be sent and summed in bfloat16 or wider, within the bound.
No kernel may reach another device: no remote copies, remote signals or barrier semaphores. Data moves between devices by JAX's collectives and lax.ppermute only.
A program may use at most 128 MiB of HBM per device.

v0:
```python
import math

import jax
import jax.numpy as jnp
from jax import lax
from jax.sharding import PartitionSpec as P

HEADS = 256
HEAD_DIM = 64
STATE = 128
GROUPS = 8
CONV = 4
BLOCK = 512
PROMPTS = 4


def passed_along(block, axis, distance):
    devices = range(lax.axis_size(axis))
    route = [(i - distance, i) for i in devices if i - distance in devices]
    return lax.ppermute(block, axis, route)


def prefix_2(value, axis, combine, identity):
    length, position = (lax.axis_size(axis), lax.axis_index(axis))
    everything = jax.tree.map(lambda part: lax.all_gather(part, axis), value)
    start = jax.tree.map(
        lambda part, zero: jnp.broadcast_to(jnp.asarray(zero, part.dtype), part.shape),
        value,
        identity,
    )

    def step(k, before):
        reached = k < position
        new = combine(before, jax.tree.map(lambda part: part[k], everything))
        return jax.tree.map(lambda a, b: jnp.where(reached, a, b), new, before)

    return lax.fori_loop(0, length, step, start)


def link(earlier, latter):
    return (earlier[0] * latter[0], latter[0][..., None, None] * earlier[1] + latter[1])


def shards(xbc, dt_raw, decay_rate, skip, conv_w, conv_b, gain, starts, assign):
    x_local, dt_local = (
        lax.all_to_all(xbc, "head", split_axis=1, concat_axis=0, tiled=True),
        lax.all_to_all(dt_raw, "head", split_axis=1, concat_axis=0, tiled=True),
    )
    rows_dev = x_local.shape[0]
    heads_loc = dt_local.shape[1]
    per_group = HEADS // GROUPS
    groups_loc = heads_loc // per_group
    width_x = per_group * HEAD_DIM
    group_w = width_x + 2 * STATE
    conv_lag = CONV - 1
    ctx_count = lax.axis_size("ctx")
    my_index = lax.axis_index("ctx")
    start_here = starts[my_index]
    rim_rows = passed_along(x_local[rows_dev - conv_lag :], "ctx", 1)
    extended = jnp.concatenate([rim_rows, x_local], 0)
    local_rows = jnp.arange(rows_dev, dtype=jnp.int32)
    summed = jnp.zeros(x_local.shape, jnp.float32) + conv_b.astype(jnp.float32)[None, :]
    for tap_idx in range(CONV):
        usable = (local_rows - conv_lag + tap_idx >= start_here) | (local_rows < start_here)
        term = extended[tap_idx : tap_idx + rows_dev] * conv_w[tap_idx].astype(jnp.float32)[None, :]
        summed = summed + jnp.where(usable[:, None], term, 0.0)
    act = jax.nn.silu(summed).astype(jnp.bfloat16).reshape(rows_dev, groups_loc, group_w)
    blocks = rows_dev // BLOCK
    values = act[:, :, :width_x].reshape(blocks, BLOCK, heads_loc, HEAD_DIM)
    b_in = act[:, :, width_x : width_x + STATE].reshape(blocks, BLOCK, groups_loc, STATE)
    c_out = act[:, :, width_x + STATE :].reshape(blocks, BLOCK, groups_loc, STATE)
    step_sizes = jax.nn.softplus(dt_local.astype(jnp.float32)).reshape(blocks, BLOCK, heads_loc)
    cumulative = jnp.cumsum(-step_sizes * decay_rate[None, None, :], 1)
    slab = math.gcd(per_group, 8)

    def block_local(block_item):
        block_vals, block_b, block_c, block_steps, block_cum = block_item
        scores = jnp.einsum("tgn,sgn->gts", block_c, block_b, preferred_element_type=jnp.float32)
        positions = jnp.arange(BLOCK, dtype=jnp.int32)
        causal = (positions[:, None] >= positions[None, :])[None]
        slab_outs = []
        for head_first in range(0, heads_loc, slab):
            group_here = head_first // per_group
            cum_slab = block_cum[:, head_first : head_first + slab].T
            log_gap = cum_slab[:, :, None] - cum_slab[:, None, :]
            weights = jnp.where(causal, jnp.exp(jnp.where(causal, log_gap, 0.0)), 0.0)
            weights = (
                weights
                * scores[group_here][None]
                * block_steps[:, head_first : head_first + slab].T[:, None, :]
            )
            slab_outs.append(
                jnp.einsum(
                    "hts,shp->thp",
                    weights.astype(jnp.bfloat16),
                    block_vals[:, head_first : head_first + slab],
                    preferred_element_type=jnp.float32,
                )
            )
        inner = jnp.concatenate(slab_outs, 1)
        end_weight = jnp.exp(block_cum[-1][None, :] - block_cum) * block_steps
        weighted = (
            (block_vals * end_weight[..., None])
            .astype(jnp.bfloat16)
            .reshape(BLOCK, groups_loc, per_group, HEAD_DIM)
        )
        fresh = jnp.einsum("sgkp,sgn->gkpn", weighted, block_b, preferred_element_type=jnp.float32)
        return (inner, fresh.reshape(heads_loc, HEAD_DIM, STATE), jnp.exp(block_cum[-1]))

    inner_all, fresh_all, decay_all = lax.map(
        block_local, (values, b_in, c_out, step_sizes, cumulative)
    )
    keep = (jnp.arange(blocks, dtype=jnp.int32) * BLOCK != start_here).astype(jnp.float32)
    zero_part = jnp.zeros((heads_loc, HEAD_DIM, STATE), jnp.float32)
    coeff = jnp.ones((heads_loc,), jnp.float32)
    mid_part = jnp.zeros_like(zero_part)
    mid_coeff = jnp.zeros_like(coeff)
    entry_parts = []
    entry_coeffs = []
    for block_idx in range(blocks):
        opened = 1.0 - keep[block_idx]
        mid_part = mid_part + opened * zero_part
        mid_coeff = mid_coeff + opened * coeff
        zero_part = zero_part * keep[block_idx]
        coeff = coeff * keep[block_idx]
        entry_parts.append(zero_part)
        entry_coeffs.append(coeff)
        zero_part = decay_all[block_idx][:, None, None] * zero_part + fresh_all[block_idx]
        coeff = decay_all[block_idx] * coeff
    prefix = prefix_2(
        (coeff, zero_part), "ctx", link, (jnp.ones_like(coeff), jnp.zeros_like(zero_part))
    )
    incoming = prefix[1]
    entering = jnp.stack(entry_parts) + jnp.stack(entry_coeffs)[..., None, None] * incoming[None]
    held = entering.astype(jnp.bfloat16).reshape(blocks, groups_loc, per_group, HEAD_DIM, STATE)
    from_state = jnp.einsum("btgn,bgkpn->btgkp", c_out, held, preferred_element_type=jnp.float32)
    from_state = (
        from_state.reshape(blocks, BLOCK, heads_loc, HEAD_DIM) * jnp.exp(cumulative)[..., None]
    )
    total = inner_all + from_state + skip[None, None, :, None] * values
    flat = total.reshape(rows_dev, groups_loc, width_x)
    mean_sq = jnp.mean(flat * flat, -1, keepdims=True)
    normed = (
        flat
        * lax.rsqrt(mean_sq + 1e-05)
        * gain.astype(jnp.float32).reshape(groups_loc, width_x)[None]
    )
    mixed = lax.all_to_all(
        normed.reshape(rows_dev, heads_loc * HEAD_DIM).astype(jnp.bfloat16),
        "head",
        split_axis=0,
        concat_axis=1,
        tiled=True,
    )
    ctx_ids = jnp.arange(ctx_count, dtype=jnp.int32)
    valid = starts < rows_dev
    before = jnp.sum(jnp.where((ctx_ids < my_index) & valid, 1, 0)).astype(jnp.int32)
    has_start = start_here < rows_dev
    mid_ok = has_start & (start_here > 0)
    after_start = starts[jnp.minimum(my_index + 1, ctx_count - 1)]
    end_ok = (my_index == ctx_count - 1) | (after_start == 0)
    mid_prompt = before - 1
    end_prompt = before + has_start.astype(jnp.int32) - 1
    mid_state = mid_part + mid_coeff[:, None, None] * incoming
    end_state = zero_part + coeff[:, None, None] * incoming
    mid_tail = lax.dynamic_slice_in_dim(
        x_local, jnp.maximum(start_here - conv_lag, 0), conv_lag, 0
    ).astype(jnp.float32)
    end_tail = x_local[rows_dev - conv_lag :].astype(jnp.float32)
    mid_dest = assign[jnp.clip(mid_prompt, 0, PROMPTS - 1)]
    end_dest = assign[jnp.clip(end_prompt, 0, PROMPTS - 1)]
    to_mid = mid_ok & (ctx_ids == mid_dest)
    to_end = end_ok & (ctx_ids == end_dest)
    send_state = jnp.where(
        to_mid[:, None, None, None],
        mid_state[None],
        jnp.where(to_end[:, None, None, None], end_state[None], 0.0),
    )
    send_tail = jnp.where(
        to_mid[:, None, None], mid_tail[None], jnp.where(to_end[:, None, None], end_tail[None], 0.0)
    )
    got_state, got_tail = (
        lax.all_to_all(send_state, "ctx", split_axis=0, concat_axis=0, tiled=True),
        lax.all_to_all(send_tail, "ctx", split_axis=0, concat_axis=0, tiled=True),
    )
    decode_states = jnp.sum(got_state, 0)[None]
    decode_tails = jnp.sum(got_tail, 0).astype(jnp.bfloat16)[None]
    return (mixed, decode_states, decode_tails)


def solution(mesh):
    in_specs = (
        P(("ctx", "head"), None),
        P(("ctx", "head"), None),
        P("head"),
        P("head"),
        P(None, "head"),
        P("head"),
        P("head"),
        P(),
        P(),
    )
    out_specs = (P(("ctx", "head"), None), P("ctx", "head", None, None), P("ctx", None, "head"))
    return jax.shard_map(shards, mesh=mesh, in_specs=in_specs, out_specs=out_specs, check_vma=False)
```

profile of v0, /device:TPU:0, one launch (start us, length us, event | category | flops | bytes accessed | tf_op | source)
XLA Modules:
  0.0 731.5 jit_solution(2749729530873529902)
XLA Ops:
  7.2 1.6 copy.88
  8.7 4.6 all-to-all-start.1
  13.4 4.9 copy.119
  18.9 4.6 all-to-all-start
  30.0 2.3 reduce-window.6
  32.5 46.3 %all-to-all-done = bf16[128,8,2304]{2,0,1:T(8,128)(2,1)} async-done(((bf16[128,8,2304]{2,0,1:T(8,128)(2,1)}), bf16[128,8,2304]{2,0,1:T(8,128)(2,1)}, u32[]{:S(2)}, u32[]{:S(2)}) %all-to-all-start) | async-done | bytes 4718624 | tf_op jit(solution)/shard_map/all_to_all | solution.py:46
  78.8 1.5 dynamic-slice_convert_fusion
  80.4 3.8 collective-permute-start
  85.6 14.3 %fusion.62 = bf16[1024,1,2304]{2,0,1:T(8,128)(2,1)S(1)} fusion(f32[2304]{0:T(1024)S(1)} %get-tuple-element.227, bf16[1024,2304]{1,0:T(8,128)(2,1)} %bitcast.25, pred[1024]{0:T(1024)(128)(4,1)S(1)} %get-tuple-element.296, f32[2304]{0:T(1024)S(1)} %get-tuple-element.228, bf16[3,2304]{1,0:T(4,128)(2,1)S(1)} %collective-permute-done, ...), kind=kLoop, calls=%fused_computation.81 | loop fusion | flops 70778880 | bytes 9501184 | tf_op jit(solution)/shard_map/reshape | solution.py:67
  100.0 2.6 slice.137
  102.6 12.9 %reshape.296 = bf16[2,512,32,64]{3,2,1,0:T(8,128)(2,1)} reshape(bf16[1024,1,2048]{2,0,1:T(8,128)(2,1)} %slice.137) | data formatting | bytes 8388608 | tf_op jit(solution)/shard_map/reshape | solution.py:69
  115.5 9.7 %copy.92 = bf16[2,512,32,64]{1,3,2,0:T(8,128)(2,1)} copy(bf16[2,512,32,64]{3,2,1,0:T(8,128)(2,1)} %reshape.296) | data formatting | bytes 8388608 | tf_op jit(solution)/shard_map/while | solution.py:110
  125.2 36.7 %while.28 = (s32[]{:T(128)}, f32[2,512,32,64]{1,3,2,0:T(8,128)}, f32[2,32,64,128]{3,2,1,0:T(8,128)S(1)}, f32[2,32]{1,0:T(2,128)S(1)}, bf16[2,512,32,64]{1,3,2,0:...) while((s32[]{:T(128)}, f32[2,512,32,64]{1,3,2,0:T(8,128)}, ...), condition=%wide.region_3.4_spmd, body=%wide.region_2.3_spmd.sunk | while | flops 1466204160 | bytes 107614104 | solution.py:110
  126.2 4.1 fusion.105
  130.3 2.9 fusion.104
  133.2 2.9 fusion.103
  136.1 2.9 fusion.102
  140.4 3.3 copy-done.1
  144.5 4.1 fusion.105
  148.6 2.9 fusion.104
  151.4 2.9 fusion.103
  154.3 2.9 fusion.102
  158.6 3.3 copy-done.1
  161.9 1.7 bitcast_multiply_fusion.1
  165.8 2.1 multiply_add_fusion.1
  175.4 1.8 select_select_fusion.1
  177.2 8.4 %all-to-all-start.4 = ((f32[16,3,2304]{2,1,0:T(4,128)}), f32[16,3,2304]{2,1,0:T(4,128)}, u32[]{:S(2)}, u32[]{:S(2)}) async-start(f32[16,3,2304]{2,1,0:T(4,128)} %select_select_fusion.1), calls=%async_computation.4 | async-start | bytes 1179648 | tf_op jit(solution)/shard_map/all_to_all | solution.py:184
  186.9 29.2 %all-gather = f32[16,1,32]{2,1,0:T(1,128)} all-gather(f32[1,1,32]{2,1,0:T(1,128)} %get-tuple-element.286), channel_id=1, replica_groups=mesh['ctx'=16,'head'=8] {'ctx'}, dimensions={0}, use_global_device_ids=true | all-gather | bytes 2176 | tf_op jit(solution)/shard_map/all_gather | solution.py:25
  216.1 70.4 %all-gather.3.cloned.1.call-done = f32[16,32,64,128]{3,2,1,0:T(8,128)} async-done(((f32[1,32,64,128]{3,2,1,0:T(8,128)}), f32[16,32,64,128]{3,2,1,0:T(8,128)}) %all-gather.3.cloned.1.call-update) | async-done | bytes 16777232 | tf_op jit(solution)/shard_map/all_gather | solution.py:25
  286.5 34.8 %while.29 = (s32[]{:T(128)}, f32[32,64,128]{2,1,0:T(8,128)S(1)}, s32[]{:T(128)}, f32[16,32]{1,0:T(8,128)}, f32[16,32,64,128]{3,2,1,0:T(8,128)}, /*index=5*/s32[]{:T(128)}, s32[]{:T(128)}) while((s32[]{:T(128)}, f32[32,64,128]{2,1,0:T(8,128)S(1)}, s32[]{:T(128)}, f32[16,32]{1,0:T(8,128)}, f32[16,32,64,128]{3,2,1,0:T(8,128)}, ...), condition=%wide.region_5.6_spmd.clone, body=%wide.region_4.5_spmd.clone.sunk | while | flops 1048580 | bytes 3146225 | solution.py:37
  293.7 1.5 fusion.108
  295.9 1.5 fusion.108
  304.6 1.5 fusion.108
  306.8 1.5 fusion.108
  317.6 1.5 fusion.108
  321.3 8.4 %multiply_reduce_fusion = (f32[2,512]{1,0:T(2,128)S(1)}, f32[2,512,32,64]{1,3,2,0:T(8,128)}) fusion(bf16[2,512,32,64]{1,3,2,0:T(8,128)(2,1)} %get-tuple-element.470, f32[32]{0:T(128)} %param.16, f32[2,512,32,64]{1,3,2,0:T(8,128)} %get-tuple-element.146, f32[2,512,32]{1,2,0:T(8,128)S(1)} %copy-done.4, bf16[2,512,128,1]{2,1,3,0:T(8,128)(2,1)S(1)} %bitcast.222, ...), kind=kOutput, calls=%fused_computation.74 | convolution fusion | flops 553122816 | bytes 23466372 | tf_op jit(solution)/shard_map/btgn,bgkpn->btgkp/dot_general | solution.py:136
  329.8 15.4 %copy.98 = f32[2,512,32,64]{1,0,3,2:T(2,128)} copy(f32[2,512,32,64]{1,3,2,0:T(8,128)} %get-tuple-element.295) | data formatting | bytes 16777216 | tf_op jit(solution)/shard_map/add | solution.py:140
  345.1 11.6 %reshape.286 = f32[8,128,2048]{1,0,2:T(8,128)} reshape(f32[2,512,32,64]{1,0,3,2:T(2,128)} %copy.98) | data formatting | bytes 16777216 | tf_op jit(solution)/shard_map/reshape | solution.py:141
  356.7 7.5 %multiply_convert_fusion.18 = bf16[8,128,2048]{1,0,2:T(8,128)(2,1)S(1)} fusion(f32[8,128,2048]{1,0,2:T(8,128)} %reshape.286, f32[2048]{0:T(1024)S(1)} %convert_element_type.112, f32[8,128]{1,0:T(8,128)S(1)} %rsqrt.12), kind=kLoop, calls=%fused_computation.73 | loop fusion | flops 6291456 | bytes 12595200 | tf_op jit(solution)/shard_map/convert_element_type | solution.py:149
  364.3 2.7 copy.99
  367.0 4.7 all-to-all-start.2
  372.7 8.6 %select_select_fusion = f32[16,32,64,128]{3,2,1,0:T(8,128)} fusion(f32[32,64,128]{2,1,0:T(8,128)S(1)} %get-tuple-element.283, f32[32,64,128]{2,1,0:T(8,128)S(1)} %get-tuple-element.282, pred[16]{0:T(512)(128)(4,1)S(1)} %copy-done.10, pred[16]{0:T(512)(128)(4,1)S(1)} %copy-done.12), kind=kLoop, calls=%fused_computation.68 | loop fusion | flops 8388608 | bytes 18874400 | tf_op jit(solution)/shard_map/jit(_where)/select_n | solution.py:174
  381.3 40.0 %all-to-all-done.2 = bf16[8,128,2048]{1,2,0:T(8,128)(2,1)} async-done(((bf16[8,128,2048]{1,2,0:T(8,128)(2,1)}), bf16[8,128,2048]{1,2,0:T(8,128)(2,1)}, u32[]{:S(2)}, u32[]{:S(2)}) %all-to-all-start.2) | async-done | bytes 4194336 | tf_op jit(solution)/shard_map/all_to_all | solution.py:148
  421.3 5.5 all-to-all-start.3
  426.8 1.8 reduce_sum.39
  428.5 6.4 copy.101
  434.9 281.0 %all-to-all-done.3 = f32[16,32,64,128]{3,2,1,0:T(8,128)} async-done(((f32[16,32,64,128]{3,2,1,0:T(8,128)}), f32[16,32,64,128]{3,2,1,0:T(8,128)}, u32[]{:S(2)}, u32[]{:S(2)}) %all-to-all-start.3) | async-done | bytes 16777248 | tf_op jit(solution)/shard_map/all_to_all | solution.py:183
  715.9 8.7 %reduce_sum.38 = f32[32,64,128]{2,1,0:T(8,128)} reduce(f32[16,32,64,128]{3,2,1,0:T(8,128)} %all-to-all-done.3, f32[]{:T(128)} %constant.87.clone.1), dimensions={0}, to_apply=%region_8.9 | reduce | flops 3932160 | bytes 17825796 | tf_op jit(solution)/shard_map/reduce_sum | solution.py:186
  (148 shorter events, 46.4 us)
Async XLA Ops:
  8.7 10.2 %all-to-all-start.1 = ((bf16[128,8,32]{0,2,1:T(8,128)(2,1)}), bf16[128,8,32]{0,2,1:T(8,128)(2,1)S(1)}, u32[]{:S(2)}, u32[]{:S(2)}) async-start(bf16[128,8,32]{0,2,1:T(8,128)(2,1)} %bitcast.28), calls=%async_computation.1 | async-start | bytes 131072 | tf_op jit(solution)/shard_map/all_to_all | solution.py:47
  13.3 10.3 %copy-start.21 = (s32[16]{0:T(128)S(1)}, s32[16]{0:T(128)}, u32[]{:S(2)}) copy-start(s32[16]{0:T(128)} %param.20) | copy-start | bytes 196
  13.3 14.5 %copy-start.8 = (bf16[2304]{0:T(1024)(128)(2,1)S(1)}, bf16[2304]{0:T(1024)(128)(2,1)}, u32[]{:S(2)}) copy-start(bf16[2304]{0:T(1024)(128)(2,1)} %param.18) | copy-start | bytes 13828
  13.3 15.8 %copy-start.5 = (bf16[4,2304]{1,0:T(4,128)(2,1)S(1)}, bf16[4,2304]{1,0:T(4,128)(2,1)}, u32[]{:S(2)}) copy-start(bf16[4,2304]{1,0:T(4,128)(2,1)} %param.17) | copy-start | bytes 55300
  13.3 16.1 %copy-start.23 = (f32[32]{0:T(128)S(1)}, f32[32]{0:T(128)}, u32[]{:S(2)}) copy-start(f32[32]{0:T(128)} %param.15) | copy-start | bytes 388
  18.9 59.9 %all-to-all-start = ((bf16[128,8,2304]{2,0,1:T(8,128)(2,1)}), bf16[128,8,2304]{2,0,1:T(8,128)(2,1)}, u32[]{:S(2)}, u32[]{:S(2)}) async-start(bf16[128,8,2304]{2,0,1:T(8,128)(2,1)} %bitcast.217), calls=%async_computation | async-start | bytes 9437184 | tf_op jit(solution)/shard_map/all_to_all | solution.py:46
  23.6 262.9 %all-gather.3.cloned.1.call-start = ((), (), s32[]{:S(2)}) async-start(), calls=%async_computation.5 | async-start | bytes 17825792 | tf_op jit(solution)/shard_map/all_gather | solution.py:25
  32.3 53.3 %copy-start.2 = (f32[2,32,4,128]{3,1,2,0:T(8,128)}, f32[2,32,4,128]{3,1,2,0:T(8,128)S(1)}, u32[]{:S(2)}) copy-start(f32[2,32,4,128]{3,1,2,0:T(8,128)S(1)} %reduce-window.6) | copy-start | bytes 393220
  32.5 70.0 %copy-start.6 = (f32[2,32,4]{1,2,0:T(4,128)}, f32[2,32,4]{1,2,0:T(4,128)S(1)}, u32[]{:S(2)}) copy-start(f32[2,32,4]{1,2,0:T(4,128)S(1)} %slice.139) | copy-start | bytes 3076
  80.4 5.2 collective-permute-start
  125.2 43.4 %copy-start.22 = (s32[16]{0:T(128)S(1)}, s32[16]{0:T(128)}, u32[]{:S(2)}) copy-start(s32[16]{0:T(128)} %param.20) | copy-start | bytes 196
  125.2 46.0 %copy-start.18 = (bf16[2048]{0:T(1024)(128)(2,1)S(1)}, bf16[2048]{0:T(1024)(128)(2,1)}, u32[]{:S(2)}) copy-start(bf16[2048]{0:T(1024)(128)(2,1)} %param.19) | copy-start | bytes 12292
  125.2 49.3 %copy-start.3 = (f32[2,32,4,128]{3,1,2,0:T(8,128)S(1)}, f32[2,32,4,128]{3,1,2,0:T(8,128)}, u32[]{:S(2)}) copy-start(f32[2,32,4,128]{3,1,2,0:T(8,128)} %copy-done.2) | copy-start | bytes 393220
  125.2 49.4 %copy-start.7 = (f32[2,32,4]{1,2,0:T(4,128)S(1)}, f32[2,32,4]{1,2,0:T(4,128)}, u32[]{:S(2)}) copy-start(f32[2,32,4]{1,2,0:T(4,128)} %copy-done.6) | copy-start | bytes 3076
  126.2 4.1 copy-start
  133.2 6.5 slice-start
  136.1 3.6 slice-start.1
  140.4 3.3 copy-start.1
  144.5 4.1 copy-start
  151.4 6.5 slice-start
  154.3 3.6 slice-start.1
  158.6 3.3 copy-start.1
  163.6 0.5 copy-start.17
  165.3 0.5 copy-start.13
  165.3 2.7 copy-start.15
  174.6 0.8 copy-start.9
  174.6 0.8 copy-start.11
  177.2 144.1 %copy-start.4 = (f32[2,512,32]{1,2,0:T(8,128)S(1)}, f32[2,512,32]{1,2,0:T(8,128)}, u32[]{:S(2)}) copy-start(f32[2,512,32]{1,2,0:T(8,128)} %fusion.71) | copy-start | bytes 393220
  177.2 189.7 %all-to-all-start.4 = ((f32[16,3,2304]{2,1,0:T(4,128)}), f32[16,3,2304]{2,1,0:T(4,128)}, u32[]{:S(2)}, u32[]{:S(2)}) async-start(f32[16,3,2304]{2,1,0:T(4,128)} %select_select_fusion.1), calls=%async_computation.4 | async-start | bytes 1179648 | tf_op jit(solution)/shard_map/all_to_all | solution.py:184
  364.2 7.4 %copy-start.14 = (f32[32]{0:T(128)S(1)}, f32[32]{0:T(128)}, u32[]{:S(2)}) copy-start(f32[32]{0:T(128)} %copy-done.13) | copy-start | bytes 388
  364.2 7.4 %copy-start.16 = (f32[32]{0:T(128)S(1)}, f32[32]{0:T(128)}, u32[]{:S(2)}) copy-start(f32[32]{0:T(128)} %copy-done.15) | copy-start | bytes 388
  364.2 7.4 %copy-start.19 = (f32[32]{0:T(128)S(1)}, f32[32]{0:T(128)}, u32[]{:S(2)}) copy-start(f32[32]{0:T(128)} %get-tuple-element.259) | copy-start | bytes 388
  364.2 7.4 %copy-start.20 = (f32[32]{0:T(128)S(1)}, f32[32]{0:T(128)}, u32[]{:S(2)}) copy-start(f32[32]{0:T(128)} %get-tuple-element.284) | copy-start | bytes 388
  366.9 5.8 copy-start.10
  366.9 5.8 copy-start.12
  367.0 54.3 %all-to-all-start.2 = ((bf16[8,128,2048]{1,2,0:T(8,128)(2,1)}), bf16[8,128,2048]{1,2,0:T(8,128)(2,1)}, u32[]{:S(2)}, u32[]{:S(2)}) async-start(bf16[8,128,2048]{1,2,0:T(8,128)(2,1)} %copy.99), calls=%async_computation.2 | async-start | bytes 8388608 | tf_op jit(solution)/shard_map/all_to_all | solution.py:148
  421.3 294.6 %all-to-all-start.3 = ((f32[16,32,64,128]{3,2,1,0:T(8,128)}), f32[16,32,64,128]{3,2,1,0:T(8,128)}, u32[]{:S(2)}, u32[]{:S(2)}) async-start(f32[16,32,64,128]{3,2,1,0:T(8,128)} %select_select_fusion), calls=%async_computation.3 | async-start | bytes 33554432 | tf_op jit(solution)/shard_map/all_to_all | solution.py:183
Sparse Core Ops, SparseCore 0:
  168.1 118.3 all-gather.2
where the time goes:
time: 743 us; the launch traced here: 731 us
  waiting for transfers between devices  440 us (59%)
  local copies, waits for them, and re-layouts  91.5 us (12%)
  other arithmetic  82.7 us (11%)
  matrix products  35.9 us (5%)
  starting transfers between devices  31.6 us (4%)
  blocking collectives  29.2 us (4%)
  between operations  20 us (3%)
    all_to_all x1, waiting for transfers between devices, shards(): lax.all_to_all(send_state, 'ctx', split_axis=0, concat_axis=0, tiled=True)  281 us
    all_gather x1, waiting for transfers between devices, prefix_2(): everything = jax.tree.map(lambda part: lax.all_gather(part, axis), value)  70.4 us
    all_to_all x1, waiting for transfers between devices, shards(): lax.all_to_all(xbc, 'head', split_axis=1, concat_axis=0, tiled=True)  46.3 us
    all_to_all x1, waiting for transfers between devices, shards(): lax.all_to_all(normed.reshape(rows_dev, heads_loc * HEAD_DIM).astype(jnp....  40 us
    all_gather x1, blocking collectives, prefix_2(): everything = jax.tree.map(lambda part: lax.all_gather(part, axis), value)  29.2 us
    dot_general x8, matrix products, block_local(): jnp.einsum('hts,shp->thp', weights.astype(jnp.bfloat16), block_vals[:, he...  25.5 us
    select_n x16, other arithmetic, step(): return jax.tree.map(lambda a, b: jnp.where(reached, a, b), new, before)  23.3 us
    add x1, local copies, waits for them, and re-layouts, shards(): total = inner_all + from_state + skip[None, None, :, None] * values  15.4 us
  transfers between devices with their start and end apart: 7, of which 6 were waited for; matrix products, arithmetic and copies ran while one was open for 16% of the time, Pallas kernels for 0%

commit v1 on v0

v1 whole, which is shorter than its diff:
```python
import functools

import jax
import jax.numpy as jnp
from jax import lax
from jax.experimental import pallas as pl
from jax.experimental.pallas import tpu as pltpu
from jax.sharding import Mesh, PartitionSpec as P

HEAD_DIM = 64
STATE = 128
GROUPS = 8
PER_GROUP = 32
WIDTH_X = PER_GROUP * HEAD_DIM
GROUP_W = WIDTH_X + 2 * STATE
LOC = GROUPS // 2
ROWS = 128
CHUNK = 2 * ROWS
CHIPS = 64
OWNERS = 16
PAY = 136
CONV = 4
LAG = CONV - 1

F32 = jnp.float32
BF16 = jnp.bfloat16


def dot(a, b, ca=1, cb=0):
    return lax.dot_general(a, b, (((ca,), (cb,)), ((), ())), preferred_element_type=F32)


def split2(v):
    hi = v.astype(BF16)
    return hi, (v - hi.astype(F32)).astype(BF16)


def spread(g):
    head = lax.broadcasted_iota(jnp.int32, (128, WIDTH_X), 0)
    col = lax.broadcasted_iota(jnp.int32, (128, WIDTH_X), 1)
    return (head == g * PER_GROUP + col // HEAD_DIM).astype(BF16)


def first_kernel(ids, starts, mine, recv, halo_a, halo_b, dt_mine, dt_recv, wts, wall,
                 pay, act, xb, score, scale, ext, bexp, bpart, lrow):
    g = pl.program_id(0)
    core = ids[0]

    @pl.when(g == 0)
    def _():
        dm, dr = dt_mine[...].astype(F32), dt_recv[...].astype(F32)
        own_first = core == 0
        raw = jnp.concatenate([jnp.where(own_first, dm, dr), jnp.where(own_first, dr, dm)], 0)
        step = jnp.log1p(jnp.exp(raw))
        decay = wall[0, 6:7, 0:128] + wall[1, 6:7, 0:128] + wall[2, 6:7, 0:128] + wall[3, 6:7, 0:128]
        cum = -step * decay
        row = lax.broadcasted_iota(jnp.int32, (CHUNK, 128), 0)
        shift = 1
        while shift < CHUNK:
            cum = cum + jnp.where(row >= shift, pltpu.roll(cum, shift, 0), 0.0)
            shift *= 2
        ahi, alo = split2(jnp.exp(cum))
        scale[0] = ahi
        scale[1] = alo
        bhi, blo = split2(jnp.exp(-cum) * step)
        bpart[0] = bhi
        bpart[1] = blo
        last = cum[CHUNK - 8 :, :]
        hi = last.astype(BF16)
        rest = last - hi.astype(F32)
        mid = rest.astype(BF16)
        low = (rest - mid.astype(F32)).astype(BF16)
        lrow[0:1] = hi.astype(F32)[7:8]
        lrow[1:2] = mid.astype(F32)[7:8]
        lrow[2:3] = low.astype(F32)[7:8]
        lrow[3:8] = jnp.zeros((5, 128), F32)

    m, r = mine[...].astype(F32), recv[...].astype(F32)
    ext[8 : 8 + ROWS, :] = jnp.where(core == 0, m, r)
    ext[8 + ROWS : 8 + CHUNK, :] = jnp.where(core == 0, r, m)
    opens = starts[ids[2]] == ids[1] * CHUNK
    halo = halo_a[...].astype(F32) + halo_b[...].astype(F32)
    ext[8 - LAG : 8, :] = jnp.where(opens, jnp.zeros_like(halo), halo)

    one_hot = spread(g)
    bexp[...] = dot(bpart[0], one_hot) + dot(bpart[1], one_hot)

    def conv(at):
        total = wts[0, CONV : CONV + 1, at] + jnp.zeros((CHUNK, 128), F32)
        for tap in range(CONV):
            total = total + ext[8 - LAG + tap : 8 - LAG + tap + CHUNK, at] * wts[0, tap : tap + 1, at]
        return (total * jax.nn.sigmoid(total)).astype(BF16)

    def strip(j, _):
        at = pl.ds(pl.multiple_of(j * 128, 128), 128)
        val = conv(at)
        act[:, at] = val
        xb[:, at] = (val.astype(F32) * bexp[:, at]).astype(BF16)
        return 0

    lax.fori_loop(0, WIDTH_X // 128, strip, 0)
    b_in = conv(pl.ds(WIDTH_X, 128))
    c_out = conv(pl.ds(WIDTH_X + STATE, 128))
    act[:, WIDTH_X : WIDTH_X + STATE] = b_in
    act[:, WIDTH_X + STATE :] = c_out
    s = dot(c_out, b_in, 1, 1)
    t_at = lax.broadcasted_iota(jnp.int32, (CHUNK, CHUNK), 0)
    s_at = lax.broadcasted_iota(jnp.int32, (CHUNK, CHUNK), 1)
    score[...] = jnp.where(s_at <= t_at, s, 0.0).astype(BF16)

    tail = ext[CHUNK : 8 + CHUNK, :]
    extra_low = lrow[...]
    for o in range(OWNERS):
        fresh = dot(b_in, xb[:, o * 128 : (o + 1) * 128], 0, 0)
        pay[0, o, 0:STATE, :] = fresh.astype(BF16)
        rows = []
        for slot in range(4):
            piece = o * 4 + slot
            tap, block = divmod(piece, GROUP_W // 128)
            if tap < LAG:
                rows.append(tail[8 - LAG + tap : 9 - LAG + tap, block * 128 : (block + 1) * 128])
            else:
                rows.append(jnp.zeros((1, 128), F32))
        pay[0, o, STATE:PAY, :] = jnp.concatenate(rows + [extra_low[0:4]], 0).astype(BF16)


def inner_kernel(score, xb, act, scale, wall, part):
    g = pl.program_id(0)
    one_hot = spread(g)
    skip = wall[0, 6:7, 128:256] + wall[1, 6:7, 128:256] + wall[2, 6:7, 128:256] + wall[3, 6:7, 128:256]
    shi = skip.astype(BF16)
    rest = skip - shi.astype(F32)
    smid = rest.astype(BF16)
    slo = (rest - smid.astype(F32)).astype(BF16)
    s = score[...]
    for j in range(0, WIDTH_X, 256):
        at = slice(j, j + 256)
        e = one_hot[:, at]
        spread_skip = sum(dot(jnp.broadcast_to(v, (8, 128)), e) for v in (shi, smid, slo))[0:1]
        spread_a = dot(scale[0], e) + dot(scale[1], e)
        part[:, at] = spread_a * dot(s, xb[:, at]) + spread_skip * act[:, at].astype(F32)


def scan_kernel(ids, starts, assign, got, held, fin, dec):
    lane = lax.broadcasted_iota(jnp.int32, (CHIPS, 128), 1)
    total = (got[:, STATE + 4, :].astype(F32) + got[:, STATE + 5, :].astype(F32)
             + got[:, STATE + 6, :].astype(F32))
    head = ids[1] * PER_GROUP + ids[2] * 2
    d0 = jnp.sum(jnp.where(lane == head, total, 0.0), 1, keepdims=True)
    d1 = jnp.sum(jnp.where(lane == head + 1, total, 0.0), 1, keepdims=True)
    dec[...] = jnp.exp(jnp.where(lane < HEAD_DIM, d0, d1))
    fin[...] = jnp.zeros_like(fin)

    def step(p, carry):
        state, count = carry
        ctx, y = p // 4, p % 4
        at = y * OWNERS + ctx
        opens = starts[ctx] == y * CHUNK
        state = jnp.where(opens, 0.0, state)
        count = count + opens.astype(jnp.int32)
        held[at] = state.astype(BF16)
        state = dec[pl.ds(at, 1), :] * (state + got[at, 0:STATE, :].astype(F32))
        nxt = jnp.minimum(p + 1, CHIPS - 1)
        ends = (p == CHIPS - 1) | (starts[nxt // 4] == (nxt % 4) * CHUNK)

        @pl.when(ends)
        def _():
            to = assign[count - 1]
            fin[to, 0:STATE, :] = state.T.astype(BF16)
            fin[to, STATE:PAY, :] = got[at, STATE:PAY, :]

        return state, count

    lax.fori_loop(0, CHIPS, step, (jnp.zeros((STATE, 128), F32), jnp.int32(0)))


def last_kernel(ids, part, act_c, scale, held, wts, out, send, y):
    g = pl.program_id(0)
    one_hot = spread(g)
    c = act_c[...]
    square = jnp.zeros((CHUNK, 128), F32)
    for o in range(0, OWNERS, 2):
        at = slice(o * 128, (o + 2) * 128)
        e = one_hot[:, at]
        h = jnp.concatenate([held[0, o], held[0, o + 1]], 1)
        total = part[:, at] + (dot(scale[0], e) + dot(scale[1], e)) * dot(c, h)
        y[:, at] = total
        square = square + total[:, :128] * total[:, :128] + total[:, 128:] * total[:, 128:]
    mean = jnp.sum(square, 1, keepdims=True) * (1.0 / WIDTH_X)
    y[:, WIDTH_X:] = jnp.broadcast_to(lax.rsqrt(mean + 1e-05), (CHUNK, 128))
    core = ids[0]
    for ref, half in ((out, core), (send, 1 - core)):
        rows = pl.ds(pl.multiple_of(half * ROWS, ROWS), ROWS)
        inv = y[rows, WIDTH_X:]
        for j in range(0, WIDTH_X, 128):
            at = slice(j, j + 128)
            ref[:, at] = (y[rows, at] * inv * wts[0, CONV + 1 : CONV + 2, at]).astype(BF16)


def place_kernel(ids, whole, recv, out):
    out[...] = recv[...]


def params(**kw):
    return pltpu.CompilerParams(dimension_semantics=("arbitrary",), **kw)


def other_groups(array, width, which):
    parts = [
        lax.dynamic_slice_in_dim(array, (2 * i + which) * width, width, 1) for i in range(LOC)
    ]
    return parts


def shards(xbc, dt_raw, decay_rate, skip, conv_w, conv_b, gain, starts, assign):
    core = lax.axis_index("core").astype(jnp.int32)
    y_at = lax.axis_index("y").astype(jnp.int32)
    ctx = (lax.axis_index("x") * 4 + lax.axis_index("z")).astype(jnp.int32)
    at = jnp.arange(4, dtype=jnp.int32)
    ids = jnp.where(at == 0, core, jnp.where(at == 1, y_at, ctx))

    swap = [(0, 1), (1, 0)]
    outgoing = jnp.concatenate(
        other_groups(xbc, GROUP_W, 1 - core) + other_groups(dt_raw, PER_GROUP, 1 - core), 1
    )
    recv = lax.ppermute(outgoing, "core", swap)
    dt_mine = jnp.concatenate(other_groups(dt_raw, PER_GROUP, core), 1)

    names = ("x", "z", "y", "core")
    rim = xbc[ROWS - LAG :]
    rims = [
        jnp.concatenate([rim[:, (2 * i + k) * GROUP_W : (2 * i + k + 1) * GROUP_W] for i in range(LOC)], 1)
        for k in range(2)
    ]
    halos = [
        lax.ppermute(rims[k], names, [(2 * p + 1, 2 * p + 2 + k) for p in range(CHIPS - 1)])
        for k in range(2)
    ]

    lanes = jnp.arange(128, dtype=jnp.int32) // PER_GROUP == y_at
    small = jnp.concatenate(
        [jnp.where(lanes, jnp.tile(decay_rate, 4), 0.0), jnp.where(lanes, jnp.tile(skip, 4), 0.0)]
    )
    table = jnp.concatenate(
        [
            conv_w.astype(F32),
            conv_b.astype(F32)[None],
            jnp.pad(gain.astype(F32), (0, GROUP_W - WIDTH_X))[None],
            jnp.pad(small, (0, GROUP_W - 256))[None],
            jnp.zeros((1, GROUP_W), F32),
        ],
        0,
    )
    wall = lax.all_to_all(jnp.broadcast_to(table[None], (4, 8, GROUP_W)), "y", 0, 0, tiled=True)

    whole_wall = pl.BlockSpec((4, 8, GROUP_W), lambda g, *_: (0, 0, 0))
    group_wall = pl.BlockSpec((1, 8, GROUP_W), lambda g, *_: (g, 0, 0))
    scale_spec = pl.BlockSpec((2, CHUNK, 128), lambda g, *_: (0, 0, 0))
    wide = lambda n: pl.BlockSpec((CHUNK, n), lambda g, *_: (0, g))

    pay, act, xb, score, scale = pl.pallas_call(
        first_kernel,
        name="first",
        grid_spec=pltpu.PrefetchScalarGridSpec(
            num_scalar_prefetch=2,
            grid=(LOC,),
            in_specs=[
                pl.BlockSpec((ROWS, GROUP_W), lambda g, ids, st: (0, 2 * g + ids[0])),
                pl.BlockSpec((ROWS, GROUP_W), lambda g, ids, st: (0, g)),
                pl.BlockSpec((LAG, GROUP_W), lambda g, ids, st: (0, g)),
                pl.BlockSpec((LAG, GROUP_W), lambda g, ids, st: (0, g)),
                pl.BlockSpec((ROWS, 128), lambda g, ids, st: (0, 0)),
                pl.BlockSpec((ROWS, 128), lambda g, ids, st: (0, LOC * GROUP_W // 128)),
                group_wall,
                whole_wall,
            ],
            out_specs=[
                pl.BlockSpec((1, OWNERS, PAY, 128), lambda g, *_: (g, 0, 0, 0)),
                wide(GROUP_W),
                wide(WIDTH_X),
                wide(CHUNK),
                scale_spec,
            ],
            scratch_shapes=[
                pltpu.VMEM((8 + CHUNK, GROUP_W), F32),
                pltpu.VMEM((CHUNK, WIDTH_X), F32),
                pltpu.VMEM((2, CHUNK, 128), BF16),
                pltpu.VMEM((8, 128), F32),
            ],
        ),
        out_shape=[
            jax.ShapeDtypeStruct((LOC, OWNERS, PAY, 128), BF16),
            jax.ShapeDtypeStruct((CHUNK, LOC * GROUP_W), BF16),
            jax.ShapeDtypeStruct((CHUNK, LOC * WIDTH_X), BF16),
            jax.ShapeDtypeStruct((CHUNK, LOC * CHUNK), BF16),
            jax.ShapeDtypeStruct((2, CHUNK, 128), BF16),
        ],
        compiler_params=params(),
        cost_estimate=pl.CostEstimate(flops=2 * 10**9, bytes_accessed=18 * 10**6, transcendentals=0),
    )(ids, starts, xbc, recv, halos[0], halos[1], dt_mine, recv, wall, wall)

    got = lax.all_to_all(pay.reshape(CHIPS, PAY, 128), ("y", "x", "z"), 0, 0, tiled=True)

    part = pl.pallas_call(
        inner_kernel,
        name="inner",
        grid=(LOC,),
        in_specs=[wide(CHUNK), wide(WIDTH_X), wide(GROUP_W), scale_spec, whole_wall],
        out_specs=wide(WIDTH_X),
        out_shape=jax.ShapeDtypeStruct((CHUNK, LOC * WIDTH_X), F32),
        compiler_params=params(),
        cost_estimate=pl.CostEstimate(flops=2 * 10**9, bytes_accessed=20 * 10**6, transcendentals=0),
    )(score, xb, act, scale, wall)

    smem = pl.BlockSpec(memory_space=pltpu.SMEM)
    vmem = pl.BlockSpec(memory_space=pltpu.VMEM)
    held, fin = pl.pallas_call(
        scan_kernel,
        name="scan",
        in_specs=[smem, smem, smem, vmem],
        out_specs=[vmem, vmem],
        out_shape=[
            jax.ShapeDtypeStruct((CHIPS, STATE, 128), BF16),
            jax.ShapeDtypeStruct((OWNERS, PAY, 128), BF16),
        ],
        scratch_shapes=[pltpu.VMEM((CHIPS, 128), F32)],
        cost_estimate=pl.CostEstimate(flops=10**7, bytes_accessed=5 * 10**6, transcendentals=0),
    )(ids, starts, assign, got)

    back = lax.all_to_all(held, ("y", "x", "z"), 0, 0, tiled=True)
    ready, fin = lax.optimization_barrier((back, fin))
    rows_got = lax.all_to_all(fin, ("x", "z"), 0, 0, tiled=True)

    out, send = pl.pallas_call(
        last_kernel,
        name="last",
        grid_spec=pltpu.PrefetchScalarGridSpec(
            num_scalar_prefetch=1,
            grid=(LOC,),
            in_specs=[
                wide(WIDTH_X),
                pl.BlockSpec((CHUNK, STATE), lambda g, ids: (0, GROUP_W // 128 * (g + 1) - 1)),
                scale_spec,
                pl.BlockSpec((1, OWNERS, STATE, 128), lambda g, ids: (g, 0, 0, 0)),
                group_wall,
            ],
            out_specs=[
                pl.BlockSpec((ROWS, WIDTH_X), lambda g, ids: (0, 2 * g + ids[0])),
                pl.BlockSpec((ROWS, WIDTH_X), lambda g, ids: (0, g)),
            ],
            scratch_shapes=[pltpu.VMEM((CHUNK, WIDTH_X + 128), F32)],
        ),
        out_shape=[
            jax.ShapeDtypeStruct((ROWS, GROUPS * WIDTH_X), BF16),
            jax.ShapeDtypeStruct((ROWS, LOC * WIDTH_X), BF16),
        ],
        compiler_params=params(),
        cost_estimate=pl.CostEstimate(flops=10**9, bytes_accessed=15 * 10**6, transcendentals=0),
    )(ids, part, act, scale, ready.reshape(LOC, OWNERS, STATE, 128), wall)

    theirs = lax.ppermute(send, "core", swap)
    mixed = pl.pallas_call(
        place_kernel,
        name="place",
        grid_spec=pltpu.PrefetchScalarGridSpec(
            num_scalar_prefetch=1,
            grid=(LOC,),
            in_specs=[
                pl.BlockSpec(memory_space=pl.ANY),
                pl.BlockSpec((ROWS, WIDTH_X), lambda g, ids: (0, g)),
            ],
            out_specs=pl.BlockSpec((ROWS, WIDTH_X), lambda g, ids: (0, 2 * g + 1 - ids[0])),
        ),
        out_shape=jax.ShapeDtypeStruct((ROWS, GROUPS * WIDTH_X), BF16),
        input_output_aliases={1: 0},
        compiler_params=params(),
    )(ids, out, theirs)

    states = rows_got[:, 0:STATE, :].astype(F32).reshape(1, PER_GROUP, HEAD_DIM, STATE)
    tails = rows_got[:, STATE : STATE + 4, :].reshape(64, 128)[: LAG * GROUP_W // 128]
    return (mixed, states, tails.reshape(1, LAG, GROUP_W))


def solution(mesh):
    axes = ("x", "z", "y", "core")
    fine = Mesh(mesh.devices.reshape(4, 4, 4, 2), axes)
    head = ("y", "core")
    in_specs = (
        P(axes, None),
        P(axes, None),
        P(head),
        P(head),
        P(None, head),
        P(head),
        P(head),
        P(),
        P(),
    )
    out_specs = (P(axes, None), P(("x", "z"), head, None, None), P(("x", "z"), None, head))
    return jax.shard_map(shards, mesh=fine, in_specs=in_specs, out_specs=out_specs, check_vma=False)
```

time: 743 us -> 165 us (0.22); the launches traced: 731 us -> 164 us
  waiting for transfers between devices: 440 us -> 25.9 us
  other arithmetic: 82.7 us -> 2.46 us
  local copies, waits for them, and re-layouts: 91.5 us -> 12.7 us
  Pallas kernels: 0 us -> 52.5 us
  matrix products: 35.9 us -> 0 us
  blocking collectives: 29.2 us -> 57 us
  starting transfers between devices: 31.6 us -> 12.4 us
  between operations: 20 us -> 0.91 us
    all_to_all x5 -> x2, waiting for transfers between devices: 368 us -> 25.9 us  [the longest x1 20.3 us: shards(): back = lax.all_to_all(held, ('y', 'x', 'z'), 0, 0, tiled=True)]
    all_gather x1 -> x0, waiting for transfers between devices: 70.4 us -> none  [prefix_2(): everything = jax.tree.map(lambda part: lax.all_gather(part, axis), value)]
    all_to_all x0 -> x2, blocking collectives: none -> 57 us  [the longest x1 41 us: shards(): lax.all_to_all(pay.reshape(CHIPS, PAY, 128), ('y', 'x', 'z'), 0, 0, tiled...]
    pallas_call x0 -> x5, Pallas kernels: none -> 52.5 us  [the longest x1 22.2 us: shards(): pl.pallas_call(first_kernel, name='first', grid_spec=pltpu.PrefetchScalar...]
    dot_general x13 -> x0, matrix products: 35.9 us -> none  [the longest x8 25.5 us: block_local(): jnp.einsum('hts,shp->thp', weights.astype(jnp.bfloat16), block_vals[:, he...]
    select_n x18 -> x2, other arithmetic: 33.7 us -> 0.58 us  [the longest x1 0.57 us: shards(): ids = jnp.where(at == 0, core, jnp.where(at == 1, y_at, ctx))]
    all_gather x1 -> x0, blocking collectives: 29.2 us -> none  [prefix_2(): everything = jax.tree.map(lambda part: lax.all_gather(part, axis), value)]
    reshape x4 -> x1, local copies, waits for them, and re-layouts: 24.7 us -> 0.62 us  [shards(): return (mixed, states, tails.reshape(1, LAG, GROUP_W))]
  transfers between devices with their start and end apart: 7 -> 6, of which waited for: 6 -> 2; matrix products, arithmetic and copies ran while one was open for 16% -> 3% of each run, Pallas kernels for 0% -> 6%
where the time goes in v1:
time: 165 us; the launch traced here: 164 us
  blocking collectives  57 us (35%)
  Pallas kernels  52.5 us (32%)
  waiting for transfers between devices  25.9 us (16%)
  local copies, waits for them, and re-layouts  12.7 us (8%)
  starting transfers between devices  12.4 us (8%)
  other arithmetic  2.46 us (1%)
    all_to_all x1, blocking collectives, shards(): lax.all_to_all(pay.reshape(CHIPS, PAY, 128), ('y', 'x', 'z'), 0, 0, tiled...  41 us
    pallas_call x1, Pallas kernels, shards(): pl.pallas_call(first_kernel, name='first', grid_spec=pltpu.PrefetchScalar...  22.2 us
    all_to_all x1, waiting for transfers between devices, shards(): back = lax.all_to_all(held, ('y', 'x', 'z'), 0, 0, tiled=True)  20.3 us
    all_to_all x1, blocking collectives, shards(): rows_got = lax.all_to_all(fin, ('x', 'z'), 0, 0, tiled=True)  16 us
    pallas_call x1, Pallas kernels, shards(): pl.pallas_call(last_kernel, name='last', grid_spec=pltpu.PrefetchScalarGr...  10.3 us
    pallas_call x1, Pallas kernels, shards(): pl.pallas_call(inner_kernel, name='inner', grid=(LOC,), in_specs=[wide(CH...  10 us
    all_to_all x1, starting transfers between devices, shards(): back = lax.all_to_all(held, ('y', 'x', 'z'), 0, 0, tiled=True)  5.83 us
    all_to_all x1, waiting for transfers between devices, shards(): lax.all_to_all(jnp.broadcast_to(table[None], (4, 8, GROUP_W)), 'y', 0, 0,...  5.56 us
  transfers between devices with their start and end apart: 6, of which 2 were waited for; matrix products, arithmetic and copies ran while one was open for 3% of the time, Pallas kernels for 6%

profile of v1, /device:TPU:0, one launch (start us, length us, event | category | flops | bytes accessed | tf_op | source)
XLA Modules:
  0.0 163.8 jit_solution(3532836363642641168)
XLA Ops:
  0.6 0.0 copy-start.4
  0.7 1.8 %constant_dynamic-slice_fusion.8 = (bf16[128,2304]{1,0:T(8,128)(2,1)S(1)}, bf16[128,2304]{1,0:T(8,128)(2,1)S(1)}, bf16[128,2304]{1,0:T(8,128)(2,1)S(1)}, bf16[128,2304]{1,0:T(8,128)(2,1)S(1)}) fusion(bf16[128,18432]{1,0:T(8,128)(2,1)} %mine.1, s32[]{:T(128)S(6)} %select_n.61, s32[]{:T(128)S(6)} %select_n.60, s32[]{:T(128)S(6)} %select_n.59, s32[]{:T(128)S(6)} %select_n.58), kind=kLoop, calls=%fused_computation.14 | loop fusion | bytes 4718608 | tf_op jit(solution)/shard_map/dynamic_slice | solution.py:210
  2.4 0.0 copy-done.4
  2.4 0.0 copy-start.11
  2.4 0.0 copy-start.12
  2.5 0.0 copy-start.10
  2.5 0.0 copy-start.9
  2.5 0.0 copy-start.8
  2.5 0.2 constant_dynamic-slice_fusion.3
  2.7 3.3 %concatenate.18 = bf16[128,9344]{1,0:T(8,128)(2,1)} concatenate(bf16[128,2304]{1,0:T(8,128)(2,1)S(1)} %get-tuple-element.36, bf16[128,2304]{1,0:T(8,128)(2,1)S(1)} %get-tuple-element.35, bf16[128,2304]{1,0:T(8,128)(2,1)S(1)} %get-tuple-element.34, bf16[128,2304]{1,0:T(8,128)(2,1)S(1)} %get-tuple-element.33, bf16[128,32]{1,0:T(8,128)(2,1)S(1)} %get-tuple-element.42, ...), dimensions={1} | concatenate | bytes 4784128 | tf_op jit(solution)/shard_map/concatenate | solution.py:223
  5.9 0.0 collective-permute-start
  5.9 1.0 fusion
  7.0 0.7 collective-permute-start.1
  7.7 0.7 collective-permute-start.2
  8.4 0.0 copy-done.11
  8.4 0.1 tile.21
  8.5 0.0 copy-done.12
  8.5 0.1 tile.9
  8.6 0.0 copy-done.10
  8.6 0.0 copy-done.9
  8.7 0.0 copy-done.8
  8.7 0.1 concatenate.23
  8.8 0.7 broadcast_in_dim.51
  9.5 5.2 %all-to-all-start = ((f32[4,8,2304]{2,1,0:T(8,128)}), f32[4,8,2304]{2,1,0:T(8,128)S(1)}, u32[]{:S(2)}, u32[]{:S(2)}) async-start(f32[4,8,2304]{2,1,0:T(8,128)} %broadcast_in_dim.51), calls=%async_computation | async-start | bytes 589824 | tf_op jit(solution)/shard_map/all_to_all | solution.py:254
  14.7 0.7 pad_maximum_fusion.2.dt_mine
  15.4 0.6 compare_select_fusion.1.ids
  16.0 0.0 collective-permute-done.1.halo_a
  16.0 0.0 collective-permute-done.2.halo_b
  16.0 5.6 %all-to-all-done.wts.wall = f32[4,8,2304]{2,1,0:T(8,128)S(1)} async-done(((f32[4,8,2304]{2,1,0:T(8,128)}), f32[4,8,2304]{2,1,0:T(8,128)S(1)}, u32[]{:S(2)}, u32[]{:S(2)}) %all-to-all-start) | async-done | bytes 294944 | tf_op jit(solution)/shard_map/all_to_all | solution.py:254
  21.5 0.0 collective-permute-done.recv.dt_recv
  21.6 0.0 copy-done.7
  21.6 0.7 copy-done.2
  22.3 1.4 copy-done
  23.7 22.2 %first.1 = (bf16[4,16,136,128]{3,2,1,0:T(8,128)(2,1)}, bf16[256,9216]{1,0:T(8,128)(2,1)}, bf16[256,8192]{1,0:T(8,128)(2,1)}, bf16[256,1024]{1,0:T(8,128)(2,1)}, bf16[2,256,128]{2,1,0:T(8,128)(2,1)}) custom-call(s32[4]{0:T(128)} %compare_select_fusion.1.ids, s32[16]{0:T(128)} %starts.3, bf16[128,18432]{1,0:T(8,128)(2,1)} %mine.1, bf16[128,9344]{1,0:T(8,128)(2,1)} %copy-done, ...), custom_call_target="tpu_custom_call" | custom-call | flops 2000000000 | bytes 18000000 | tf_op jit(solution)/shard_map/first/pallas_call | solution.py:261
  45.9 41.0 %all_to_all.20.got = bf16[64,136,128]{2,1,0:T(8,128)(2,1)} all-to-all(bf16[64,136,128]{2,1,0:T(8,128)(2,1)} %bitcast.6), channel_id=1, replica_groups=mesh['x'=4,'z'=4,'y'=4,'core'=2] {'y','x','z'}, dimensions={0} | all-to-all | bytes 4456448 | tf_op jit(solution)/shard_map/all_to_all | solution.py:302
  86.9 5.5 %scan.1 = (bf16[64,128,128]{2,1,0:T(8,128)(2,1)}, bf16[16,136,128]{2,1,0:T(8,128)(2,1)}) custom-call(s32[4]{0:T(128)} %compare_select_fusion.1.ids, s32[16]{0:T(128)} %starts.3, s32[4]{0:T(128)} %assign.1, bf16[64,136,128]{2,1,0:T(8,128)(2,1)} %all_to_all.20.got), custom_call_target="tpu_custom_call" | custom-call | flops 10000000 | bytes 5000000 | tf_op jit(solution)/shard_map/scan/pallas_call | solution.py:317
  92.5 5.8 %all-to-all-start.2 = ((bf16[64,128,128]{2,1,0:T(8,128)(2,1)}), bf16[64,128,128]{2,1,0:T(8,128)(2,1)S(1)}, u32[]{:S(2)}, u32[]{:S(2)}) async-start(bf16[64,128,128]{2,1,0:T(8,128)(2,1)} %get-tuple-element.19), calls=%async_computation.2 | async-start | bytes 4194304 | tf_op jit(solution)/shard_map/all_to_all | solution.py:330
  98.3 10.0 %inner.1.part = f32[256,8192]{1,0:T(8,128)} custom-call(bf16[256,1024]{1,0:T(8,128)(2,1)} %get-tuple-element.14.score, bf16[256,8192]{1,0:T(8,128)(2,1)} %get-tuple-element.15.xb, bf16[256,9216]{1,0:T(8,128)(2,1)} %get-tuple-element.16.act.act_c, bf16[2,256,128]{2,1,0:T(8,128)(2,1)} %get-tuple-element.17.scale, f32[4,8,2304]{2,1,0:T(8,128)} %copy-done.2), custom_call_target="tpu_custom_call" | custom-call | flops 2000000000 | bytes 20000000 | tf_op jit(solution)/shard_map/inner/pallas_call | solution.py:304
  108.3 20.3 %all-to-all-done.2 = bf16[64,128,128]{2,1,0:T(8,128)(2,1)S(1)} async-done(((bf16[64,128,128]{2,1,0:T(8,128)(2,1)}), bf16[64,128,128]{2,1,0:T(8,128)(2,1)S(1)}, u32[]{:S(2)}, u32[]{:S(2)}) %all-to-all-start.2) | async-done | bytes 2097184 | tf_op jit(solution)/shard_map/all_to_all | solution.py:330
  128.6 1.3 copy-done.1
  129.9 10.3 %last.1 = (bf16[128,16384]{1,0:T(8,128)(2,1)}, bf16[128,8192]{1,0:T(8,128)(2,1)}) custom-call(s32[4]{0:T(128)} %compare_select_fusion.1.ids, f32[256,8192]{1,0:T(8,128)} %inner.1.part, bf16[256,9216]{1,0:T(8,128)(2,1)} %get-tuple-element.16.act.act_c, bf16[2,256,128]{2,1,0:T(8,128)(2,1)} %get-tuple-element.17.scale, bf16[4,16,128,128]{3,2,1,0:T(8,128)(2,1)} %bitcast.5, ...), custom_call_target="tpu_custom_call" | custom-call | flops 1000000000 | bytes 15000000 | tf_op jit(solution)/shard_map/last/pallas_call | solution.py:334
  140.2 0.0 collective-permute-start.3
  140.2 16.0 %all_to_all.21 = bf16[16,136,128]{2,1,0:T(8,128)(2,1)S(1)} all-to-all(bf16[16,136,128]{2,1,0:T(8,128)(2,1)S(1)} %copy-done.5), channel_id=1, replica_groups=mesh['x'=4,'z'=4,'y'=4,'core'=2] {'x','z'}, dimensions={0} | all-to-all | bytes 1114112 | tf_op jit(solution)/shard_map/all_to_all | solution.py:332
  156.3 1.1 convert.5
  157.4 0.6 reshape.32
  158.0 0.0 collective-permute-done.3.recv
  158.0 1.3 copy-done.3
  159.3 4.4 %place.1 = bf16[128,16384]{1,0:T(8,128)(2,1)} custom-call(s32[4]{0:T(128)} %compare_select_fusion.1.ids, bf16[128,16384]{1,0:T(8,128)(2,1)} %get-tuple-element.22.whole, bf16[128,8192]{1,0:T(8,128)(2,1)} %copy-done.3), custom_call_target="tpu_custom_call", output_to_operand_aliasing={{}: (1, {})} | custom-call | tf_op jit(solution)/shard_map/place/pallas_call | solution.py:362
  (23 shorter events, 0.2 us)
Async XLA Ops:
  0.6 1.8 %copy-start.4 = (bf16[128,256]{1,0:T(8,128)(2,1)S(1)}, bf16[128,256]{1,0:T(8,128)(2,1)}, u32[]{:S(2)}) copy-start(bf16[128,256]{1,0:T(8,128)(2,1)} %param.10) | copy-start | bytes 196612
  2.4 5.9 %copy-start.11 = (f32[32]{0:T(128)S(1)}, f32[32]{0:T(128)}, u32[]{:S(2)}) copy-start(f32[32]{0:T(128)} %param.12) | copy-start | bytes 388
  2.4 6.0 %copy-start.12 = (f32[32]{0:T(128)S(1)}, f32[32]{0:T(128)}, u32[]{:S(2)}) copy-start(f32[32]{0:T(128)} %param.11) | copy-start | bytes 388
  2.5 6.1 %copy-start.10 = (bf16[2048]{0:T(1024)(128)(2,1)S(1)}, bf16[2048]{0:T(1024)(128)(2,1)}, u32[]{:S(2)}) copy-start(bf16[2048]{0:T(1024)(128)(2,1)} %param.15) | copy-start | bytes 12292
  2.5 6.2 %copy-start.9 = (bf16[2304]{0:T(1024)(128)(2,1)S(1)}, bf16[2304]{0:T(1024)(128)(2,1)}, u32[]{:S(2)}) copy-start(bf16[2304]{0:T(1024)(128)(2,1)} %param.14) | copy-start | bytes 13828
  2.5 6.2 %copy-start.8 = (bf16[4,2304]{1,0:T(4,128)(2,1)S(1)}, bf16[4,2304]{1,0:T(4,128)(2,1)}, u32[]{:S(2)}) copy-start(bf16[4,2304]{1,0:T(4,128)(2,1)} %param.13) | copy-start | bytes 55300
  5.9 15.6 %collective-permute-start = (bf16[128,9344]{1,0:T(8,128)(2,1)}, bf16[128,9344]{1,0:T(8,128)(2,1)S(1)}, u32[]{:S(2)}, u32[]{:S(2)}) collective-permute-start(bf16[128,9344]{1,0:T(8,128)(2,1)} %concatenate.18), channel_id=1, source_target_pairs={{0,1},{1,0},{2,3},{3,2},{4,5},{5,4},{6,7},{7,6},{8,9},{9,8},{10,11... | collective-permute-start | bytes 7176200 | tf_op jit(solution)/shard_map/ppermute | solution.py:226
  7.0 9.0 %collective-permute-start.1 = (bf16[3,9216]{1,0:T(4,128)(2,1)S(1)}, bf16[3,9216]{1,0:T(4,128)(2,1)S(1)}, u32[]{:S(2)}, u32[]{:S(2)}) collective-permute-start(bf16[3,9216]{1,0:T(4,128)(2,1)S(1)} %pad_maximum_fusion), channel_id=1, source_target_pairs={{1,2},{3,4},{5,6},{7,8},{9,10},{11,12},{13,14},{15,16},{17,18},{19... | collective-permute-start | bytes 165896 | tf_op jit(solution)/shard_map/ppermute | solution.py:236
  7.7 8.3 %collective-permute-start.2 = (bf16[3,9216]{1,0:T(4,128)(2,1)S(1)}, bf16[3,9216]{1,0:T(4,128)(2,1)S(1)}, u32[]{:S(2)}, u32[]{:S(2)}) collective-permute-start(bf16[3,9216]{1,0:T(4,128)(2,1)S(1)} %pad_maximum_fusion.1), channel_id=1, source_target_pairs={{1,3},{3,5},{5,7},{7,9},{9,11},{11,13},{13,15},{15,17},{17,19},{19... | collective-permute-start | bytes 165896 | tf_op jit(solution)/shard_map/ppermute | solution.py:236
  9.5 12.1 %all-to-all-start = ((f32[4,8,2304]{2,1,0:T(8,128)}), f32[4,8,2304]{2,1,0:T(8,128)S(1)}, u32[]{:S(2)}, u32[]{:S(2)}) async-start(f32[4,8,2304]{2,1,0:T(8,128)} %broadcast_in_dim.51), calls=%async_computation | async-start | bytes 589824 | tf_op jit(solution)/shard_map/all_to_all | solution.py:254
  16.0 5.6 %copy-start.6 = (bf16[3,9216]{1,0:T(4,128)(2,1)}, bf16[3,9216]{1,0:T(4,128)(2,1)S(1)}, u32[]{:S(2)}) copy-start(bf16[3,9216]{1,0:T(4,128)(2,1)S(1)} %collective-permute-done.1.halo_a) | copy-start | bytes 165892
  16.0 5.6 %copy-start.7 = (bf16[3,9216]{1,0:T(4,128)(2,1)}, bf16[3,9216]{1,0:T(4,128)(2,1)S(1)}, u32[]{:S(2)}) copy-start(bf16[3,9216]{1,0:T(4,128)(2,1)S(1)} %collective-permute-done.2.halo_b) | copy-start | bytes 165892
  21.5 0.7 copy-start.2
  22.3 1.4 copy-start
  92.5 36.1 %all-to-all-start.2 = ((bf16[64,128,128]{2,1,0:T(8,128)(2,1)}), bf16[64,128,128]{2,1,0:T(8,128)(2,1)S(1)}, u32[]{:S(2)}, u32[]{:S(2)}) async-start(bf16[64,128,128]{2,1,0:T(8,128)(2,1)} %get-tuple-element.19), calls=%async_computation.2 | async-start | bytes 4194304 | tf_op jit(solution)/shard_map/all_to_all | solution.py:330
  128.6 1.3 copy-start.1
  129.9 10.3 %copy-start.5 = (bf16[16,136,128]{2,1,0:T(8,128)(2,1)S(1)}, bf16[16,136,128]{2,1,0:T(8,128)(2,1)}, u32[]{:S(2)}) copy-start(bf16[16,136,128]{2,1,0:T(8,128)(2,1)} %get-tuple-element.24) | copy-start | bytes 1671172
  140.2 17.8 %collective-permute-start.3 = (bf16[128,8192]{1,0:T(8,128)(2,1)}, bf16[128,8192]{1,0:T(8,128)(2,1)S(1)}, u32[]{:S(2)}, u32[]{:S(2)}) collective-permute-start(bf16[128,8192]{1,0:T(8,128)(2,1)} %get-tuple-element.23), channel_id=1, source_target_pairs={{0,1},{1,0},{2,3},{3,2},{4,5},{5,4},{6,7},{7,6},{8,9},{9,8},{10,11... | collective-permute-start | bytes 6291464 | tf_op jit(solution)/shard_map/ppermute | solution.py:361
  158.0 1.3 copy-start.3

commit v2 on v1

v2 whole, which is shorter than its diff:
```python
import jax
import jax.numpy as jnp
from jax import lax
from jax.experimental import pallas as pl
from jax.experimental.pallas import tpu as pltpu
from jax.sharding import Mesh, PartitionSpec as P


HEAD_DIM = 64
STATE = 128
GROUPS = 8
PER_GROUP = 32
WIDTH_X = PER_GROUP * HEAD_DIM
GROUP_W = WIDTH_X + 2 * STATE
LOC = GROUPS // 2
ROWS = 128
CHUNK = 2 * ROWS
CHIPS = 64
OWNERS = 16
PAY = 136
CONV = 4
LAG = CONV - 1

F32 = jnp.float32
BF16 = jnp.bfloat16


def dot(a, b, ca=1, cb=0):
    return lax.dot_general(a, b, (((ca,), (cb,)), ((), ())), preferred_element_type=F32)


def pack3(v):
    lane = lax.broadcasted_iota(jnp.int32, v.shape, 1)
    hi = v.astype(BF16).astype(F32)
    mid = (v - hi).astype(BF16).astype(F32)
    low = (v - hi - mid).astype(BF16).astype(F32)
    three = jnp.where(lane < 32, hi, jnp.where(lane < 64, pltpu.roll(mid, 32, 1), pltpu.roll(low, 64, 1)))
    return jnp.where(lane < 96, three, 0.0).astype(BF16)


def spread():
    row = lax.broadcasted_iota(jnp.int32, (128, WIDTH_X), 0)
    col = lax.broadcasted_iota(jnp.int32, (128, WIDTH_X), 1)
    return ((row & 31) == (col >> 6)).astype(F32).astype(BF16)


def first_kernel(ids, starts, mine, recv, rim_a, rim_b, dt_mine, dt_recv, tab0, tab1, tab2, tab3,
                 pay, act, xb, score, scale, tabs, ext, bexp, one_hot, afull, bfull, lrow, small):
    g = pl.program_id(0)
    core = ids[0]
    own = pl.multiple_of(core * ROWS, ROWS)
    other = pl.multiple_of((1 - core) * ROWS, ROWS)

    @pl.when(g == 0)
    def _():
        col = lax.broadcasted_iota(jnp.int32, (2 * 128, 128), 0)
        lane = lax.broadcasted_iota(jnp.int32, (2 * 128, 128), 1)
        pick = (col == ((2 * (lane >> 5) + core) << 5) + (lane & 31)).astype(F32).astype(BF16)
        afull[pl.ds(own, ROWS), :] = dot(dt_mine[...], pick)
        afull[pl.ds(other, ROWS), :] = dot(dt_recv[...], pick)
        step = jnp.log1p(jnp.exp(afull[...]))
        small[...] = tab0[6:7, 0:256] + tab1[6:7, 0:256] + tab2[6:7, 0:256] + tab3[6:7, 0:256]
        cum = -step * small[:, 0:128]
        row = lax.broadcasted_iota(jnp.int32, (CHUNK, 128), 0)
        shift = 1
        while shift < CHUNK:
            cum = cum + jnp.where(row >= shift, pltpu.roll(cum, shift, 0), 0.0)
            shift *= 2
        afull[...] = jnp.exp(cum)
        bfull[...] = jnp.exp(-cum) * step
        last = cum[CHUNK - 8 :, :]
        hi = last.astype(BF16).astype(F32)
        mid = (last - hi).astype(BF16).astype(F32)
        low = (last - hi - mid).astype(BF16).astype(F32)
        lrow[0:1] = hi[7:8]
        lrow[1:2] = mid[7:8]
        lrow[2:3] = low[7:8]
        lrow[3:8] = jnp.zeros((5, 128), F32)
        one_hot[...] = spread()

    shift = (ids[1] - g) & 3
    table = jnp.where(
        shift == 0, tab0[...], jnp.where(shift == 1, tab1[...], jnp.where(shift == 2, tab2[...], tab3[...]))
    )
    tabs[0] = table
    tabs[0, 7:8, 0:256] = small[...]

    back = (128 - g * PER_GROUP) & 127
    scale[0] = pack3(pltpu.roll(afull[...], back, 1))
    bexp[...] = dot(pack3(pltpu.roll(bfull[...], back, 1)), one_hot[...])
    opens = starts[ids[2]] == ids[1] * CHUNK

    def conv(j):
        at = pl.ds(pl.multiple_of(j * 128, 128), 128)
        halo = rim_a[:, at].astype(F32) + rim_b[:, at].astype(F32)
        ext[j, 8 - LAG : 8, :] = jnp.where(opens, jnp.zeros_like(halo), halo)
        ext[j, pl.ds(8 + own, ROWS), :] = mine[:, at].astype(F32)
        ext[j, pl.ds(8 + other, ROWS), :] = recv[:, at].astype(F32)
        total = tabs[0, CONV : CONV + 1, at] + jnp.zeros((CHUNK, 128), F32)
        for tap in range(CONV):
            total = total + ext[j, 8 - LAG + tap : 8 - LAG + tap + CHUNK, :] * tabs[0, tap : tap + 1, at]
        half = 0.5 * total
        return at, (half * jnp.tanh(half) + half).astype(BF16)

    def strip(j, _):
        at, val = conv(j)
        act[:, at] = val
        xb[:, at] = (val.astype(F32) * bexp[:, at]).astype(BF16)
        return 0

    lax.fori_loop(0, WIDTH_X // 128, strip, 0)
    _, b_in = conv(WIDTH_X // 128)
    _, c_out = conv(WIDTH_X // 128 + 1)
    act[:, WIDTH_X : WIDTH_X + STATE] = b_in
    act[:, WIDTH_X + STATE :] = c_out
    s = dot(c_out, b_in, 1, 1)
    t_at = lax.broadcasted_iota(jnp.int32, (CHUNK, CHUNK), 0)
    s_at = lax.broadcasted_iota(jnp.int32, (CHUNK, CHUNK), 1)
    score[...] = jnp.where(s_at <= t_at, s, 0.0).astype(BF16)

    b_t = b_in.astype(F32).T.astype(BF16)
    for o in range(0, OWNERS, 2):
        fresh = dot(b_t, xb[:, o * 128 : (o + 2) * 128]).astype(BF16)
        pay[0, o, 0:STATE, :] = fresh[:, :128]
        pay[0, o + 1, 0:STATE, :] = fresh[:, 128:]
    for o in range(OWNERS):
        rows = []
        for slot in range(4):
            tap, block = divmod(o * 4 + slot, GROUP_W // 128)
            if tap < LAG:
                end = 8 + CHUNK - LAG + tap
                rows.append(ext[block, end : end + 1, :])
            else:
                rows.append(jnp.zeros((1, 128), F32))
        pay[0, o, STATE:PAY, :] = jnp.concatenate(rows + [lrow[0:4]], 0).astype(BF16)


def inner_kernel(score, xb, act, scale, tabs, part, one_hot):
    @pl.when(pl.program_id(0) == 0)
    def _():
        one_hot[...] = spread()

    back = (128 - pl.program_id(0) * PER_GROUP) & 127
    skip = pack3(pltpu.roll(jnp.broadcast_to(tabs[0, 7:8, 128:256], (8, 128)), back, 1))
    s = score[...]
    for j in range(0, WIDTH_X, 256):
        at = slice(j, j + 256)
        e = one_hot[:, at]
        part[:, at] = dot(scale[0], e) * dot(s, xb[:, at]) + dot(skip, e)[0:1] * act[:, at].astype(F32)


def scan_kernel(ids, starts, assign, got, held, fin, dec):
    lane = lax.broadcasted_iota(jnp.int32, (CHIPS, 128), 1)
    total = (got[:, STATE + 4, :].astype(F32) + got[:, STATE + 5, :].astype(F32)
             + got[:, STATE + 6, :].astype(F32))
    head = ids[1] * PER_GROUP + ids[2] * 2
    d0 = jnp.sum(jnp.where(lane == head, total, 0.0), 1, keepdims=True)
    d1 = jnp.sum(jnp.where(lane == head + 1, total, 0.0), 1, keepdims=True)
    dec[...] = jnp.exp(jnp.where(lane < HEAD_DIM, d0, d1))
    fin[...] = jnp.zeros_like(fin)

    def step(ctx, carry):
        state, count = carry
        for y in range(4):
            at = y * OWNERS + ctx
            opens = starts[ctx] == y * CHUNK
            state = jnp.where(opens, 0.0, state)
            count = count + opens.astype(jnp.int32)
            held[at] = state.astype(BF16)
            state = dec[pl.ds(at, 1), :] * (state + got[at, 0:STATE, :].astype(F32))
            if y < 3:
                ends = starts[ctx] == (y + 1) * CHUNK
            else:
                ends = (ctx == OWNERS - 1) | (starts[jnp.minimum(ctx + 1, OWNERS - 1)] == 0)

            @pl.when(ends)
            def _():
                to = assign[count - 1]
                fin[to, 0:STATE, :] = state.T.astype(BF16)
                fin[to, STATE:PAY, :] = got[at, STATE:PAY, :]

        return state, count

    lax.fori_loop(0, OWNERS, step, (jnp.zeros((STATE, 128), F32), jnp.int32(0)))


def last_kernel(ids, part, act_c, scale, held, tabs, out, y, one_hot):
    @pl.when(pl.program_id(0) == 0)
    def _():
        one_hot[...] = spread()

    c = act_c[...]
    square = jnp.zeros((ROWS, 128), F32)
    for o in range(0, OWNERS, 2):
        at = slice(o * 128, (o + 2) * 128)
        h = jnp.concatenate([held[0, o], held[0, o + 1]], 1)
        total = part[:, at] + dot(scale[0], one_hot[:, at]) * dot(c, h)
        y[:, at] = total
        square = square + total[:, :128] * total[:, :128] + total[:, 128:] * total[:, 128:]
    mean = jnp.sum(square, 1, keepdims=True) * (1.0 / WIDTH_X)
    inv = jnp.broadcast_to(lax.rsqrt(mean + 1e-05), (ROWS, 128))
    for j in range(0, WIDTH_X, 128):
        at = slice(j, j + 128)
        out[:, at] = (y[:, at] * inv * tabs[0, CONV + 1 : CONV + 2, at]).astype(BF16)


def place_kernel(ids, whole, recv, out):
    out[...] = recv[...]


def params():
    return pltpu.CompilerParams(dimension_semantics=("arbitrary",), vmem_limit_bytes=24 * 2**20)


def wide(n):
    return pl.BlockSpec((CHUNK, n), lambda g, *_: (0, g))


TABLE = pl.BlockSpec((1, 8, GROUP_W), lambda g, *_: (g, 0, 0))


def last_call(ids, part, act, scale, held, tabs, own):
    half = (lambda ids: ids[0]) if own else (lambda ids: 1 - ids[0])
    cols = (lambda g, ids: 2 * g + ids[0]) if own else (lambda g, ids: g)
    width = (GROUPS if own else LOC) * WIDTH_X
    return pl.pallas_call(
        last_kernel,
        name="last",
        grid_spec=pltpu.PrefetchScalarGridSpec(
            num_scalar_prefetch=1,
            grid=(LOC,),
            in_specs=[
                pl.BlockSpec((ROWS, WIDTH_X), lambda g, ids: (half(ids), g)),
                pl.BlockSpec((ROWS, STATE), lambda g, ids: (half(ids), GROUP_W // 128 * (g + 1) - 1)),
                pl.BlockSpec((1, ROWS, 128), lambda g, ids: (g, half(ids), 0)),
                pl.BlockSpec((1, OWNERS, STATE, 128), lambda g, ids: (g, 0, 0, 0)),
                TABLE,
            ],
            out_specs=pl.BlockSpec((ROWS, WIDTH_X), lambda g, ids: (0, cols(g, ids))),
            scratch_shapes=[pltpu.VMEM((ROWS, WIDTH_X), F32), pltpu.VMEM((128, WIDTH_X), BF16)],
        ),
        out_shape=jax.ShapeDtypeStruct((ROWS, width), BF16),
        compiler_params=params(),
        cost_estimate=pl.CostEstimate(flops=10**9, bytes_accessed=9 * 10**6, transcendentals=0),
    )(ids, part, act, scale, held, tabs)


def shards(xbc, dt_raw, decay_rate, skip, conv_w, conv_b, gain, starts, assign):
    core = lax.axis_index("core").astype(jnp.int32)
    y_at = lax.axis_index("y").astype(jnp.int32)
    ctx = (lax.axis_index("x") * 4 + lax.axis_index("z")).astype(jnp.int32)
    at = jnp.arange(4, dtype=jnp.int32)
    ids = jnp.where(at == 0, core, jnp.where(at == 1, y_at, ctx))

    swap = [(0, 1), (1, 0)]
    recv = lax.ppermute(xbc, "core", swap)
    dt_recv = lax.ppermute(dt_raw, "core", swap)

    names = ("x", "z", "y", "core")
    rim = xbc[ROWS - LAG :]
    rims = [
        lax.ppermute(rim, names, [(2 * p + 1, 2 * p + 2 + k) for p in range(CHIPS - 1)])
        for k in range(2)
    ]

    lanes = jnp.arange(128, dtype=jnp.int32) // PER_GROUP == y_at
    small = jnp.concatenate(
        [jnp.where(lanes, jnp.tile(decay_rate, 4), 0.0), jnp.where(lanes, jnp.tile(skip, 4), 0.0)]
    )
    table = jnp.concatenate(
        [
            conv_w.astype(F32),
            conv_b.astype(F32)[None],
            jnp.pad(gain.astype(F32), (0, GROUP_W - WIDTH_X))[None],
            jnp.pad(small, (0, GROUP_W - 256))[None],
            jnp.zeros((1, GROUP_W), F32),
        ],
        0,
    )
    tables = [table] + [
        lax.ppermute(table, "y", [(i, (i + s) % 4) for i in range(4)]) for s in range(1, 4)
    ]

    whole_table = pl.BlockSpec((8, GROUP_W), lambda g, *_: (0, 0))
    rows_spec = pl.BlockSpec((ROWS, GROUP_W), lambda g, ids, st: (0, 2 * g + ids[0]))
    rim_spec = pl.BlockSpec((LAG, GROUP_W), lambda g, ids, st: (0, 2 * g + ids[0]))
    dt_spec = pl.BlockSpec((ROWS, 256), lambda g, ids, st: (0, 0))
    scale_spec = pl.BlockSpec((1, CHUNK, 128), lambda g, *_: (g, 0, 0))

    pay, act, xb, score, scale, tabs = pl.pallas_call(
        first_kernel,
        name="first",
        grid_spec=pltpu.PrefetchScalarGridSpec(
            num_scalar_prefetch=2,
            grid=(LOC,),
            in_specs=[rows_spec] * 2 + [rim_spec] * 2 + [dt_spec] * 2 + [whole_table] * 4,
            out_specs=[
                pl.BlockSpec((1, OWNERS, PAY, 128), lambda g, *_: (g, 0, 0, 0)),
                wide(GROUP_W),
                wide(WIDTH_X),
                wide(CHUNK),
                scale_spec,
                TABLE,
            ],
            scratch_shapes=[
                pltpu.VMEM((GROUP_W // 128, 8 + CHUNK, 128), F32),
                pltpu.VMEM((CHUNK, WIDTH_X), F32),
                pltpu.VMEM((128, WIDTH_X), BF16),
                pltpu.VMEM((CHUNK, 128), F32),
                pltpu.VMEM((CHUNK, 128), F32),
                pltpu.VMEM((8, 128), F32),
                pltpu.VMEM((1, 256), F32),
            ],
        ),
        out_shape=[
            jax.ShapeDtypeStruct((LOC, OWNERS, PAY, 128), BF16),
            jax.ShapeDtypeStruct((CHUNK, LOC * GROUP_W), BF16),
            jax.ShapeDtypeStruct((CHUNK, LOC * WIDTH_X), BF16),
            jax.ShapeDtypeStruct((CHUNK, LOC * CHUNK), BF16),
            jax.ShapeDtypeStruct((LOC, CHUNK, 128), BF16),
            jax.ShapeDtypeStruct((LOC, 8, GROUP_W), F32),
        ],
        compiler_params=params(),
        cost_estimate=pl.CostEstimate(flops=2 * 10**9, bytes_accessed=18 * 10**6, transcendentals=0),
    )(ids, starts, xbc, recv, *rims, dt_raw, dt_recv, *tables)

    got = lax.all_to_all(pay.reshape(CHIPS, PAY, 128), ("y", "x", "z"), 0, 0, tiled=True)

    part = pl.pallas_call(
        inner_kernel,
        name="inner",
        grid=(LOC,),
        in_specs=[wide(CHUNK), wide(WIDTH_X), wide(GROUP_W), scale_spec, TABLE],
        out_specs=wide(WIDTH_X),
        out_shape=jax.ShapeDtypeStruct((CHUNK, LOC * WIDTH_X), F32),
        scratch_shapes=[pltpu.VMEM((128, WIDTH_X), BF16)],
        compiler_params=params(),
        cost_estimate=pl.CostEstimate(flops=2 * 10**9, bytes_accessed=20 * 10**6, transcendentals=0),
    )(score, xb, act, scale, tabs)

    smem = pl.BlockSpec(memory_space=pltpu.SMEM)
    vmem = pl.BlockSpec(memory_space=pltpu.VMEM)
    held, fin = pl.pallas_call(
        scan_kernel,
        name="scan",
        in_specs=[smem, smem, smem, vmem],
        out_specs=[vmem, vmem],
        out_shape=[
            jax.ShapeDtypeStruct((CHIPS, STATE, 128), BF16),
            jax.ShapeDtypeStruct((OWNERS, PAY, 128), BF16),
        ],
        scratch_shapes=[pltpu.VMEM((CHIPS, 128), F32)],
        compiler_params=pltpu.CompilerParams(vmem_limit_bytes=24 * 2**20),
        cost_estimate=pl.CostEstimate(flops=10**7, bytes_accessed=5 * 10**6, transcendentals=0),
    )(ids, starts, assign, got)

    back = lax.all_to_all(held, ("y", "x", "z"), 0, 0, tiled=True)
    back, fin = lax.optimization_barrier((back, fin))
    rows_got = lax.all_to_all(fin, ("x", "z"), 0, 0, tiled=True)

    back = back.reshape(LOC, OWNERS, STATE, 128)
    send = last_call(ids, part, act, scale, back, tabs, False)
    theirs = lax.ppermute(send, "core", swap)
    out = last_call(ids, part, act, scale, back, tabs, True)
    mixed = pl.pallas_call(
        place_kernel,
        name="place",
        grid_spec=pltpu.PrefetchScalarGridSpec(
            num_scalar_prefetch=1,
            grid=(LOC,),
            in_specs=[
                pl.BlockSpec(memory_space=pl.ANY),
                pl.BlockSpec((ROWS, WIDTH_X), lambda g, ids: (0, g)),
            ],
            out_specs=pl.BlockSpec((ROWS, WIDTH_X), lambda g, ids: (0, 2 * g + 1 - ids[0])),
        ),
        out_shape=jax.ShapeDtypeStruct((ROWS, GROUPS * WIDTH_X), BF16),
        input_output_aliases={1: 0},
        compiler_params=params(),
    )(ids, out, theirs)

    states = rows_got[:, 0:STATE, :].astype(F32).reshape(1, PER_GROUP, HEAD_DIM, STATE)
    tails = rows_got[:, STATE : STATE + 4, :].reshape(64, 128)[: LAG * GROUP_W // 128]
    return (mixed, states, tails.reshape(1, LAG, GROUP_W))


def solution(mesh):
    axes = ("x", "z", "y", "core")
    fine = Mesh(mesh.devices.reshape(4, 4, 4, 2), axes)
    head = ("y", "core")
    in_specs = (
        P(axes, None),
        P(axes, None),
        P(head),
        P(head),
        P(None, head),
        P(head),
        P(head),
        P(),
        P(),
    )
    out_specs = (P(axes, None), P(("x", "z"), head, None, None), P(("x", "z"), None, head))
    return jax.shard_map(shards, mesh=fine, in_specs=in_specs, out_specs=out_specs, check_vma=False)
```

time: 165 us -> 157 us (0.952)
  local copies, waits for them, and re-layouts: 12.7 us -> 33.1 us
  Pallas kernels: 52.5 us -> 35.8 us
  blocking collectives: 57 us -> 46.5 us
  waiting for transfers between devices: 25.9 us -> 20.3 us
  starting transfers between devices: 12.4 us -> 17.7 us
    unnamed x26 -> x28, local copies, waits for them, and re-layouts: 4.82 us -> 26.6 us
    all_to_all x1 -> x0, blocking collectives: 16 us -> none  [shards(): rows_got = lax.all_to_all(fin, ('x', 'z'), 0, 0, tiled=True)]
    pallas_call x1, Pallas kernels: 22.2 us -> 14.2 us  [shards(): pl.pallas_call(first_kernel, name='first', grid_spec=pltpu.PrefetchScalar...]
    ppermute x3 -> x7, starting transfers between devices: 1.33 us -> 7.64 us  [the longest x3 6 us: shards(): lax.ppermute(table, 'y', [(i, (i + s) % 4) for i in range(4)])]
    all_to_all x1, blocking collectives: 41 us -> 46.5 us  [shards(): lax.all_to_all(pay.reshape(CHIPS, PAY, 128), ('y', 'x', 'z'), 0, 0, tiled...]
    pallas_call x1, Pallas kernels: 10 us -> 5.46 us  [shards(): pl.pallas_call(inner_kernel, name='inner', grid=(LOC,), in_specs=[wide(CH...]
    concatenate x1 -> x0, local copies, waits for them, and re-layouts: 3.28 us -> none  [shards(): jnp.concatenate(other_groups(xbc, GROUP_W, 1 - core) + other_groups(dt_ra...]
    all_to_all x1, waiting for transfers between devices: 20.3 us -> 17 us  [shards(): back = lax.all_to_all(held, ('y', 'x', 'z'), 0, 0, tiled=True)]
  transfers between devices with their start and end apart: 6 -> 10, of which waited for: 2 -> 4; matrix products, arithmetic and copies ran while one was open for 3% -> 5% of each run, Pallas kernels for 6% -> 6%
where the time goes in v2:
time: 157 us; the launch traced here: 156 us
  blocking collectives  46.5 us (30%)
  Pallas kernels  35.8 us (23%)
  local copies, waits for them, and re-layouts  33.1 us (21%)
  waiting for transfers between devices  20.3 us (13%)
  starting transfers between devices  17.7 us (11%)
  other arithmetic  1.8 us (1%)
    all_to_all x1, blocking collectives, shards(): lax.all_to_all(pay.reshape(CHIPS, PAY, 128), ('y', 'x', 'z'), 0, 0, tiled...  46.5 us
    unnamed x28, local copies, waits for them, and re-layouts  26.6 us
    all_to_all x1, waiting for transfers between devices, shards(): back = lax.all_to_all(held, ('y', 'x', 'z'), 0, 0, tiled=True)  17 us
    pallas_call x1, Pallas kernels, shards(): pl.pallas_call(first_kernel, name='first', grid_spec=pltpu.PrefetchScalar...  14.2 us
    pallas_call x2, Pallas kernels, last_call(): pl.pallas_call(last_kernel, name='last', grid_spec=pltpu.PrefetchScalarGr...  8.91 us
    ppermute x3, starting transfers between devices, shards(): lax.ppermute(table, 'y', [(i, (i + s) % 4) for i in range(4)])  6 us
    all_to_all x1, starting transfers between devices, shards(): back = lax.all_to_all(held, ('y', 'x', 'z'), 0, 0, tiled=True)  5.86 us
    pallas_call x1, Pallas kernels, shards(): pl.pallas_call(inner_kernel, name='inner', grid=(LOC,), in_specs=[wide(CH...  5.46 us
  transfers between devices with their start and end apart: 10, of which 4 were waited for; matrix products, arithmetic and copies ran while one was open for 5% of the time, Pallas kernels for 6%

profile of v2, /device:TPU:0, one launch (start us, length us, event | category | flops | bytes accessed | tf_op | source)
XLA Modules:
  0.0 156.0 jit_solution(7736257704234278561)
XLA Ops:
  0.6 0.1 collective-permute-start
  0.7 0.7 tile.20
  1.4 0.1 tile.21
  1.5 0.7 tile.8
  2.1 0.1 tile.9
  2.2 0.7 pad_convert_fusion
  3.0 0.7 reshape.32
  3.7 0.8 concatenate.7.tab0
  4.5 1.8 %collective-permute-start.4 = (f32[8,2304]{1,0:T(8,128)S(1)}, f32[8,2304]{1,0:T(8,128)S(1)}, u32[]{:S(2)}, u32[]{:S(2)}) collective-permute-start(f32[8,2304]{1,0:T(8,128)S(1)} %concatenate.7.tab0), channel_id=1, source_target_pairs={{0,2},{2,4},{4,6},{6,0},{1,3},{3,5},{5,7},{7,1},{8,10},{10,12},{12... | collective-permute-start | bytes 221192 | tf_op jit(solution)/shard_map/ppermute | solution.py:281
  6.2 0.2 collective-permute-start.3
  6.4 2.9 %collective-permute-start.5 = (f32[8,2304]{1,0:T(8,128)S(1)}, f32[8,2304]{1,0:T(8,128)S(1)}, u32[]{:S(2)}, u32[]{:S(2)}) collective-permute-start(f32[8,2304]{1,0:T(8,128)S(1)} %concatenate.7.tab0), channel_id=1, source_target_pairs={{0,4},{2,6},{4,0},{6,2},{1,5},{3,7},{5,1},{7,3},{8,12},{10,14},{12... | collective-permute-start | bytes 221192 | tf_op jit(solution)/shard_map/ppermute | solution.py:281
  9.3 1.3 collective-permute-start.6
  10.7 1.0 slice.12
  11.7 0.0 collective-permute-done.3.dt_recv
  11.7 0.7 collective-permute-start.1
  12.4 0.0 collective-permute-done.4.tab1
  12.4 0.7 collective-permute-start.2
  13.1 0.2 collective-permute-done.5.tab2
  13.3 0.3 collective-permute-done.6.tab3
  13.7 0.0 collective-permute-done.1.rim_a
  13.7 0.0 copy-start.7
  13.7 2.3 %copy-done.7 = bf16[128,18432]{1,0:T(8,128)(2,1)S(1)} copy-done((bf16[128,18432]{1,0:T(8,128)(2,1)S(1)}, bf16[128,18432]{1,0:T(8,128)(2,1)}, u32[]{:S(2)}) %copy-start.7) | copy-done | bytes 4718616
  16.0 0.8 copy-done.11
  16.9 0.7 copy-done.12
  17.5 14.2 %first.1 = (bf16[4,16,136,128]{3,2,1,0:T(8,128)(2,1)S(1)}, bf16[256,9216]{1,0:T(8,128)(2,1)S(1)}, bf16[256,8192]{1,0:T(8,128)(2,1)S(1)}, bf16[256,1024]{1,0:T(8,...) custom-call(s32[4]{0:T(128)S(1)} %compare_select_fusion.1.ids, s32[16]{0:T(128)S(1)} %copy-done.12, ...), custom_call_target="tpu_custom_call" | custom-call | flops 2000000000 | bytes 18000000 | tf_op jit(solution)/shard_map/first/pallas_call | solution.py:290
  31.7 2.2 %copy-done.3 = bf16[256,9216]{1,0:T(8,128)(2,1)} copy-done((bf16[256,9216]{1,0:T(8,128)(2,1)}, bf16[256,9216]{1,0:T(8,128)(2,1)S(1)}, u32[]{:S(2)}) %copy-start.3) | copy-done | bytes 4718616
  34.0 46.5 %all_to_all.15.got = bf16[64,136,128]{2,1,0:T(8,128)(2,1)S(1)} all-to-all(bf16[64,136,128]{2,1,0:T(8,128)(2,1)S(1)} %bitcast.7), channel_id=1, replica_groups=mesh['x'=4,'z'=4,'y'=4,'core'=2] {'y','x','z'}, dimensions={0} | all-to-all | bytes 4456448 | tf_op jit(solution)/shard_map/all_to_all | solution.py:327
  80.5 2.9 %scan.1 = (bf16[64,128,128]{2,1,0:T(8,128)(2,1)S(1)}, bf16[16,136,128]{2,1,0:T(8,128)(2,1)}) custom-call(s32[4]{0:T(128)S(1)} %compare_select_fusion.1.ids, s32[16]{0:T(128)S(1)} %copy-done.12, s32[4]{0:T(128)S(1)} %copy-done.13, bf16[64,136,128]{2,1,0:T(8,128)(2,1)S(1)} %all_to_all.15.got), custom_call_target="tpu_custom_call" | custom-call | flops 10000000 | bytes 5000000 | tf_op jit(solution)/shard_map/scan/pallas_call | solution.py:343
  83.4 1.3 copy-done.10
  84.7 5.9 %all-to-all-start.1 = ((bf16[64,128,128]{2,1,0:T(8,128)(2,1)}), bf16[64,128,128]{2,1,0:T(8,128)(2,1)S(1)}, u32[]{:S(2)}, u32[]{:S(2)}) async-start(bf16[64,128,128]{2,1,0:T(8,128)(2,1)} %copy-done.10), calls=%async_computation.1 | async-start | bytes 4194304 | tf_op jit(solution)/shard_map/all_to_all | solution.py:357
  90.5 2.3 %copy-done.4 = bf16[256,9216]{1,0:T(8,128)(2,1)S(1)} copy-done((bf16[256,9216]{1,0:T(8,128)(2,1)S(1)}, bf16[256,9216]{1,0:T(8,128)(2,1)}, u32[]{:S(2)}) %copy-start.4) | copy-done | bytes 4718616
  92.9 2.2 %copy-done.9 = bf16[256,8192]{1,0:T(8,128)(2,1)S(1)} copy-done((bf16[256,8192]{1,0:T(8,128)(2,1)S(1)}, bf16[256,8192]{1,0:T(8,128)(2,1)}, u32[]{:S(2)}) %copy-start.9) | copy-done | bytes 4194328
  95.0 5.5 %inner.1.part = f32[256,8192]{1,0:T(8,128)S(1)} custom-call(bf16[256,1024]{1,0:T(8,128)(2,1)S(1)} %get-tuple-element.13.score, bf16[256,8192]{1,0:T(8,128)(2,1)S(1)} %copy-done.9, bf16[256,9216]{1,0:T(8,128)(2,1)S(1)} %copy-done.4, bf16[4,256,128]{2,1,0:T(8,128)(2,1)S(1)} %get-tuple-element.16.scale, f32[4,8,2304]{2,1,0:T(8,128)S(1)} %get-tuple-element.17.tabs), custom_call_target="tpu_custom_call" | custom-call | flops 2000000000 | bytes 20000000 | tf_op jit(solution)/shard_map/inner/pallas_call | solution.py:329
  100.5 3.3 %copy-done = f32[256,8192]{1,0:T(8,128)} copy-done((f32[256,8192]{1,0:T(8,128)}, f32[256,8192]{1,0:T(8,128)S(1)}, u32[]{:S(2)}) %copy-start) | copy-done | bytes 8388632
  103.8 17.0 %all-to-all-done.1 = bf16[64,128,128]{2,1,0:T(8,128)(2,1)S(1)} async-done(((bf16[64,128,128]{2,1,0:T(8,128)(2,1)}), bf16[64,128,128]{2,1,0:T(8,128)(2,1)S(1)}, u32[]{:S(2)}, u32[]{:S(2)}) %all-to-all-start.1) | async-done | bytes 2097184 | tf_op jit(solution)/shard_map/all_to_all | solution.py:357
  120.8 3.4 %copy-done.1 = f32[256,8192]{1,0:T(8,128)S(1)} copy-done((f32[256,8192]{1,0:T(8,128)S(1)}, f32[256,8192]{1,0:T(8,128)}, u32[]{:S(2)}) %copy-start.1) | copy-done | bytes 8388632
  124.2 2.3 %copy-done.5 = bf16[256,9216]{1,0:T(8,128)(2,1)S(1)} copy-done((bf16[256,9216]{1,0:T(8,128)(2,1)S(1)}, bf16[256,9216]{1,0:T(8,128)(2,1)}, u32[]{:S(2)}) %copy-start.5) | copy-done | bytes 4718616
  126.6 4.5 %last.3 = bf16[128,8192]{1,0:T(8,128)(2,1)} custom-call(s32[4]{0:T(128)S(1)} %compare_select_fusion.1.ids, f32[256,8192]{1,0:T(8,128)S(1)} %copy-done.1, bf16[256,9216]{1,0:T(8,128)(2,1)S(1)} %copy-done.5, bf16[4,256,128]{2,1,0:T(8,128)(2,1)S(1)} %get-tuple-element.16.scale, bf16[4,16,128,128]{3,2,1,0:T(8,128)(2,1)S(1)} %bitcast.5, ...), custom_call_target="tpu_custom_call" | custom-call | flops 1000000000 | bytes 9000000 | tf_op jit(solution)/shard_map/last/pallas_call | solution.py:226
  131.1 4.2 %all-to-all-start.2 = ((bf16[16,136,128]{2,1,0:T(8,128)(2,1)}), bf16[16,136,128]{2,1,0:T(8,128)(2,1)}, u32[]{:S(2)}, u32[]{:S(2)}) async-start(bf16[16,136,128]{2,1,0:T(8,128)(2,1)} %get-tuple-element.22), calls=%async_computation.2 | async-start | bytes 1114112 | tf_op jit(solution)/shard_map/all_to_all | solution.py:359
  135.3 3.4 %copy-done.2 = f32[256,8192]{1,0:T(8,128)S(1)} copy-done((f32[256,8192]{1,0:T(8,128)S(1)}, f32[256,8192]{1,0:T(8,128)}, u32[]{:S(2)}) %copy-start.2) | copy-done | bytes 8388632
  138.7 2.3 %copy-done.6 = bf16[256,9216]{1,0:T(8,128)(2,1)S(1)} copy-done((bf16[256,9216]{1,0:T(8,128)(2,1)S(1)}, bf16[256,9216]{1,0:T(8,128)(2,1)}, u32[]{:S(2)}) %copy-start.6) | copy-done | bytes 4718616
  141.0 4.4 %last.2.whole = bf16[128,16384]{1,0:T(8,128)(2,1)} custom-call(s32[4]{0:T(128)S(1)} %compare_select_fusion.1.ids, f32[256,8192]{1,0:T(8,128)S(1)} %copy-done.2, bf16[256,9216]{1,0:T(8,128)(2,1)S(1)} %copy-done.6, bf16[4,256,128]{2,1,0:T(8,128)(2,1)S(1)} %get-tuple-element.16.scale, bf16[4,16,128,128]{3,2,1,0:T(8,128)(2,1)S(1)} %bitcast.6, ...), custom_call_target="tpu_custom_call" | custom-call | flops 1000000000 | bytes 9000000 | tf_op jit(solution)/shard_map/last/pallas_call | solution.py:226
  145.4 2.7 %all-to-all-done.2 = bf16[16,136,128]{2,1,0:T(8,128)(2,1)} async-done(((bf16[16,136,128]{2,1,0:T(8,128)(2,1)}), bf16[16,136,128]{2,1,0:T(8,128)(2,1)}, u32[]{:S(2)}, u32[]{:S(2)}) %all-to-all-start.2) | async-done | bytes 557088 | tf_op jit(solution)/shard_map/all_to_all | solution.py:359
  148.1 1.1 slice.16
  149.2 1.1 convert.5
  150.3 0.8 slice.17
  151.1 0.6 reshape.31
  151.7 4.3 %place.1 = bf16[128,16384]{1,0:T(8,128)(2,1)} custom-call(s32[4]{0:T(128)S(1)} %compare_select_fusion.1.ids, bf16[128,16384]{1,0:T(8,128)(2,1)} %last.2.whole, bf16[128,8192]{1,0:T(8,128)(2,1)} %collective-permute-done.7.recv), custom_call_target="tpu_custom_call", output_to_operand_aliasing={{}: (1, {})} | custom-call | tf_op jit(solution)/shard_map/place/pallas_call | solution.py:365
  (26 shorter events, 0.1 us)
Async XLA Ops:
  0.6 13.1 %collective-permute-start = (bf16[128,18432]{1,0:T(8,128)(2,1)}, bf16[128,18432]{1,0:T(8,128)(2,1)}, u32[]{:S(2)}, u32[]{:S(2)}) collective-permute-start(bf16[128,18432]{1,0:T(8,128)(2,1)} %mine.1), channel_id=1, source_target_pairs={{0,1},{1,0},{2,3},{3,2},{4,5},{5,4},{6,7},{7,6},{8,9},{9,8},{10,11... | collective-permute-start | bytes 14155784 | tf_op jit(solution)/shard_map/ppermute | solution.py:256
  4.5 8.0 %collective-permute-start.4 = (f32[8,2304]{1,0:T(8,128)S(1)}, f32[8,2304]{1,0:T(8,128)S(1)}, u32[]{:S(2)}, u32[]{:S(2)}) collective-permute-start(f32[8,2304]{1,0:T(8,128)S(1)} %concatenate.7.tab0), channel_id=1, source_target_pairs={{0,2},{2,4},{4,6},{6,0},{1,3},{3,5},{5,7},{7,1},{8,10},{10,12},{12... | collective-permute-start | bytes 221192 | tf_op jit(solution)/shard_map/ppermute | solution.py:281
  6.2 5.5 %collective-permute-start.3 = (bf16[128,256]{1,0:T(8,128)(2,1)}, bf16[128,256]{1,0:T(8,128)(2,1)S(1)}, u32[]{:S(2)}, u32[]{:S(2)}) collective-permute-start(bf16[128,256]{1,0:T(8,128)(2,1)} %dt_mine.1), channel_id=1, source_target_pairs={{0,1},{1,0},{2,3},{3,2},{4,5},{5,4},{6,7},{7,6},{8,9},{9,8},{10,11... | collective-permute-start | bytes 196616 | tf_op jit(solution)/shard_map/ppermute | solution.py:257
  6.4 6.9 %collective-permute-start.5 = (f32[8,2304]{1,0:T(8,128)S(1)}, f32[8,2304]{1,0:T(8,128)S(1)}, u32[]{:S(2)}, u32[]{:S(2)}) collective-permute-start(f32[8,2304]{1,0:T(8,128)S(1)} %concatenate.7.tab0), channel_id=1, source_target_pairs={{0,4},{2,6},{4,0},{6,2},{1,5},{3,7},{5,1},{7,3},{8,12},{10,14},{12... | collective-permute-start | bytes 221192 | tf_op jit(solution)/shard_map/ppermute | solution.py:281
  9.3 4.4 %collective-permute-start.6 = (f32[8,2304]{1,0:T(8,128)S(1)}, f32[8,2304]{1,0:T(8,128)S(1)}, u32[]{:S(2)}, u32[]{:S(2)}) collective-permute-start(f32[8,2304]{1,0:T(8,128)S(1)} %concatenate.7.tab0), channel_id=1, source_target_pairs={{0,6},{2,0},{4,2},{6,4},{1,7},{3,1},{5,3},{7,5},{8,14},{10,8},{12,... | collective-permute-start | bytes 221192 | tf_op jit(solution)/shard_map/ppermute | solution.py:281
  11.7 1.9 %collective-permute-start.1 = (bf16[3,18432]{1,0:T(4,128)(2,1)S(1)}, bf16[3,18432]{1,0:T(4,128)(2,1)S(1)}, u32[]{:S(2)}, u32[]{:S(2)}) collective-permute-start(bf16[3,18432]{1,0:T(4,128)(2,1)S(1)} %slice.12), channel_id=1, source_target_pairs={{1,2},{3,4},{5,6},{7,8},{9,10},{11,12},{13,14},{15,16},{17,18},{19... | collective-permute-start | bytes 331784 | tf_op jit(solution)/shard_map/ppermute | solution.py:262
  12.4 1.3 collective-permute-start.2
  13.7 2.3 %copy-start.7 = (bf16[128,18432]{1,0:T(8,128)(2,1)S(1)}, bf16[128,18432]{1,0:T(8,128)(2,1)}, u32[]{:S(2)}) copy-start(bf16[128,18432]{1,0:T(8,128)(2,1)} %mine.1) | copy-start | bytes 14155780
  16.0 0.8 copy-start.11
  16.9 0.7 copy-start.12
  31.7 2.2 %copy-start.3 = (bf16[256,9216]{1,0:T(8,128)(2,1)}, bf16[256,9216]{1,0:T(8,128)(2,1)S(1)}, u32[]{:S(2)}) copy-start(bf16[256,9216]{1,0:T(8,128)(2,1)S(1)} %get-tuple-element.15.act.act_c) | copy-start | bytes 14155780
  34.0 49.4 %copy-start.8 = (bf16[256,8192]{1,0:T(8,128)(2,1)}, bf16[256,8192]{1,0:T(8,128)(2,1)S(1)}, u32[]{:S(2)}) copy-start(bf16[256,8192]{1,0:T(8,128)(2,1)S(1)} %get-tuple-element.14.xb) | copy-start | bytes 12582916
  34.0 46.5 %copy-start.13 = (s32[4]{0:T(128)S(1)}, s32[4]{0:T(128)}, u32[]{:S(2)}) copy-start(s32[4]{0:T(128)} %assign.1) | copy-start | bytes 52
  83.4 1.3 copy-start.10
  84.7 36.2 %all-to-all-start.1 = ((bf16[64,128,128]{2,1,0:T(8,128)(2,1)}), bf16[64,128,128]{2,1,0:T(8,128)(2,1)S(1)}, u32[]{:S(2)}, u32[]{:S(2)}) async-start(bf16[64,128,128]{2,1,0:T(8,128)(2,1)} %copy-done.10), calls=%async_computation.1 | async-start | bytes 4194304 | tf_op jit(solution)/shard_map/all_to_all | solution.py:357
  90.5 2.3 %copy-start.4 = (bf16[256,9216]{1,0:T(8,128)(2,1)S(1)}, bf16[256,9216]{1,0:T(8,128)(2,1)}, u32[]{:S(2)}) copy-start(bf16[256,9216]{1,0:T(8,128)(2,1)} %copy-done.3) | copy-start | bytes 14155780
  92.9 2.2 %copy-start.9 = (bf16[256,8192]{1,0:T(8,128)(2,1)S(1)}, bf16[256,8192]{1,0:T(8,128)(2,1)}, u32[]{:S(2)}) copy-start(bf16[256,8192]{1,0:T(8,128)(2,1)} %copy-done.8) | copy-start | bytes 12582916
  100.5 3.3 %copy-start = (f32[256,8192]{1,0:T(8,128)}, f32[256,8192]{1,0:T(8,128)S(1)}, u32[]{:S(2)}) copy-start(f32[256,8192]{1,0:T(8,128)S(1)} %inner.1.part) | copy-start | bytes 25165828
  120.8 3.4 %copy-start.1 = (f32[256,8192]{1,0:T(8,128)S(1)}, f32[256,8192]{1,0:T(8,128)}, u32[]{:S(2)}) copy-start(f32[256,8192]{1,0:T(8,128)} %copy-done) | copy-start | bytes 25165828
  124.2 2.3 %copy-start.5 = (bf16[256,9216]{1,0:T(8,128)(2,1)S(1)}, bf16[256,9216]{1,0:T(8,128)(2,1)}, u32[]{:S(2)}) copy-start(bf16[256,9216]{1,0:T(8,128)(2,1)} %copy-done.3) | copy-start | bytes 14155780
  131.1 20.6 %collective-permute-start.7 = (bf16[128,8192]{1,0:T(8,128)(2,1)}, bf16[128,8192]{1,0:T(8,128)(2,1)}, u32[]{:S(2)}, u32[]{:S(2)}) collective-permute-start(bf16[128,8192]{1,0:T(8,128)(2,1)} %last.3), channel_id=1, source_target_pairs={{0,1},{1,0},{2,3},{3,2},{4,5},{5,4},{6,7},{7,6},{8,9},{9,8},{10,11... | collective-permute-start | bytes 6291464 | tf_op jit(solution)/shard_map/ppermute | solution.py:363
  131.1 17.1 %all-to-all-start.2 = ((bf16[16,136,128]{2,1,0:T(8,128)(2,1)}), bf16[16,136,128]{2,1,0:T(8,128)(2,1)}, u32[]{:S(2)}, u32[]{:S(2)}) async-start(bf16[16,136,128]{2,1,0:T(8,128)(2,1)} %get-tuple-element.22), calls=%async_computation.2 | async-start | bytes 1114112 | tf_op jit(solution)/shard_map/all_to_all | solution.py:359
  135.3 3.4 %copy-start.2 = (f32[256,8192]{1,0:T(8,128)S(1)}, f32[256,8192]{1,0:T(8,128)}, u32[]{:S(2)}) copy-start(f32[256,8192]{1,0:T(8,128)} %copy-done) | copy-start | bytes 25165828
  138.7 2.3 %copy-start.6 = (bf16[256,9216]{1,0:T(8,128)(2,1)S(1)}, bf16[256,9216]{1,0:T(8,128)(2,1)}, u32[]{:S(2)}) copy-start(bf16[256,9216]{1,0:T(8,128)(2,1)} %copy-done.3) | copy-start | bytes 14155780

commit v3 on v2

--- a/solution.py
+++ b/solution.py
@@ -44,8 +44,19 @@
     return ((row & 31) == (col >> 6)).astype(F32).astype(BF16)
 
 
+def table_kernel(conv_w, conv_b, gain, decay, skip, rows, table, rim):
+    table[0:CONV] = 0.5 * conv_w[...].astype(F32)
+    table[CONV : CONV + 1] = 0.5 * conv_b[...].astype(F32).reshape(1, GROUP_W)
+    table[CONV + 1 : CONV + 2, 0:WIDTH_X] = gain[...].astype(F32).reshape(1, WIDTH_X)
+    table[CONV + 1 : CONV + 2, WIDTH_X:] = jnp.zeros((1, GROUP_W - WIDTH_X), F32)
+    table[CONV + 2 :] = jnp.zeros((8 - CONV - 2, GROUP_W), F32)
+    d, s = decay[...].reshape(1, PER_GROUP), skip[...].reshape(1, PER_GROUP)
+    table[CONV + 2 : CONV + 3, 0:256] = jnp.concatenate([d] * 4 + [s] * 4, 1)
+    rim[...] = rows[...].astype(F32)[16 - LAG :].astype(BF16)
+
+
 def first_kernel(ids, starts, mine, recv, rim_a, rim_b, dt_mine, dt_recv, tab0, tab1, tab2, tab3,
-                 pay, act, xb, score, scale, tabs, ext, bexp, one_hot, afull, bfull, lrow, small):
+                 pay, act, xb, score, scale, tabs, ext, one_hot, afull, bfull, lrow, small, bnow):
     g = pl.program_id(0)
     core = ids[0]
     own = pl.multiple_of(core * ROWS, ROWS)
@@ -59,8 +70,12 @@
         afull[pl.ds(own, ROWS), :] = dot(dt_mine[...], pick)
         afull[pl.ds(other, ROWS), :] = dot(dt_recv[...], pick)
         step = jnp.log1p(jnp.exp(afull[...]))
-        small[...] = tab0[6:7, 0:256] + tab1[6:7, 0:256] + tab2[6:7, 0:256] + tab3[6:7, 0:256]
-        cum = -step * small[:, 0:128]
+        block = (lax.broadcasted_iota(jnp.int32, (1, 256), 1) >> 5) & 3
+        every = jnp.zeros((1, 256), F32)
+        for shift, tab in enumerate((tab0, tab1, tab2, tab3)):
+            every = every + jnp.where(block == ((ids[1] - shift) & 3), tab[6:7, 0:256], 0.0)
+        small[...] = every
+        cum = -step * every[:, 0:128]
         row = lax.broadcasted_iota(jnp.int32, (CHUNK, 128), 0)
         shift = 1
         while shift < CHUNK:
@@ -87,7 +102,7 @@
 
     back = (128 - g * PER_GROUP) & 127
     scale[0] = pack3(pltpu.roll(afull[...], back, 1))
-    bexp[...] = dot(pack3(pltpu.roll(bfull[...], back, 1)), one_hot[...])
+    bnow[...] = pack3(pltpu.roll(bfull[...], back, 1))
     opens = starts[ids[2]] == ids[1] * CHUNK
 
     def conv(j):
@@ -96,33 +111,40 @@
         ext[j, 8 - LAG : 8, :] = jnp.where(opens, jnp.zeros_like(halo), halo)
         ext[j, pl.ds(8 + own, ROWS), :] = mine[:, at].astype(F32)
         ext[j, pl.ds(8 + other, ROWS), :] = recv[:, at].astype(F32)
-        total = tabs[0, CONV : CONV + 1, at] + jnp.zeros((CHUNK, 128), F32)
-        for tap in range(CONV):
-            total = total + ext[j, 8 - LAG + tap : 8 - LAG + tap + CHUNK, :] * tabs[0, tap : tap + 1, at]
-        half = 0.5 * total
+        half = tabs[0, CONV : CONV + 1, at] + ext[j, 8 - LAG : 8 - LAG + CHUNK, :] * tabs[0, 0:1, at]
+        for tap in range(1, CONV):
+            half = half + ext[j, 8 - LAG + tap : 8 - LAG + tap + CHUNK, :] * tabs[0, tap : tap + 1, at]
         return at, (half * jnp.tanh(half) + half).astype(BF16)
 
-    def strip(j, _):
+    strips = WIDTH_X // 128
+    _, b_in = conv(strips)
+    _, c_out = conv(strips + 1)
+    act[:, WIDTH_X : WIDTH_X + STATE] = b_in
+    act[:, WIDTH_X + STATE :] = c_out
+    b_t = b_in.astype(F32).T.astype(BF16)
+
+    def weigh(j):
         at, val = conv(j)
         act[:, at] = val
-        xb[:, at] = (val.astype(F32) * bexp[:, at]).astype(BF16)
+        xb[:, at] = (val.astype(F32) * dot(bnow[...], one_hot[:, at])).astype(BF16)
+
+    def fresh(j):
+        at = pl.ds(pl.multiple_of(j * 128, 128), 128)
+        pay[0, j, 0:STATE, :] = dot(b_t, xb[:, at]).astype(BF16)
+
+    weigh(0)
+
+    def strip(j, _):
+        fresh(j - 1)
+        weigh(j)
         return 0
 
-    lax.fori_loop(0, WIDTH_X // 128, strip, 0)
-    _, b_in = conv(WIDTH_X // 128)
-    _, c_out = conv(WIDTH_X // 128 + 1)
-    act[:, WIDTH_X : WIDTH_X + STATE] = b_in
-    act[:, WIDTH_X + STATE :] = c_out
+    lax.fori_loop(1, strips, strip, 0)
+    fresh(strips - 1)
     s = dot(c_out, b_in, 1, 1)
     t_at = lax.broadcasted_iota(jnp.int32, (CHUNK, CHUNK), 0)
     s_at = lax.broadcasted_iota(jnp.int32, (CHUNK, CHUNK), 1)
     score[...] = jnp.where(s_at <= t_at, s, 0.0).astype(BF16)
-
-    b_t = b_in.astype(F32).T.astype(BF16)
-    for o in range(0, OWNERS, 2):
-        fresh = dot(b_t, xb[:, o * 128 : (o + 2) * 128]).astype(BF16)
-        pay[0, o, 0:STATE, :] = fresh[:, :128]
-        pay[0, o + 1, 0:STATE, :] = fresh[:, 128:]
     for o in range(OWNERS):
         rows = []
         for slot in range(4):
@@ -204,12 +226,39 @@
         out[:, at] = (y[:, at] * inv * tabs[0, CONV + 1 : CONV + 2, at]).astype(BF16)
 
 
-def place_kernel(ids, whole, recv, out):
-    out[...] = recv[...]
-
-
-def params():
-    return pltpu.CompilerParams(dimension_semantics=("arbitrary",), vmem_limit_bytes=24 * 2**20)
+def place_kernel(ids, whole, theirs, out, held, sem_in, sem_out):
+    def loads(g):
+        cols = pl.ds(g * WIDTH_X, WIDTH_X)
+        return pltpu.make_async_copy(theirs.at[:, cols], held.at[g], sem_in.at[g])
+
+    def stores(g):
+        cols = pl.ds(pl.multiple_of((2 * g + 1 - ids[0]) * WIDTH_X, WIDTH_X), WIDTH_X)
+        return pltpu.make_async_copy(held.at[g], out.at[:, cols], sem_out.at[g])
+
+    for g in range(LOC):
+        loads(g).start()
+    for g in range(LOC):
+        loads(g).wait()
+        stores(g).start()
+    for g in range(LOC):
+        stores(g).wait()
+
+
+def rows_kernel(got, states, tails):
+    states[...] = got[:, 0:STATE, :].astype(F32)
+    for piece in range(LAG * GROUP_W // 128):
+        tap, block = divmod(piece, GROUP_W // 128)
+        row = STATE + piece % 4
+        tails[0, tap : tap + 1, block * 128 : (block + 1) * 128] = got[piece // 4, row : row + 1, :]
+
+
+FIRST, INNER, SCAN, LAST, PLACE, EXTRA, SMALL = 52, 52, 52, 52, 44, 52, 60
+
+
+def params(grant, *semantics):
+    return pltpu.CompilerParams(
+        dimension_semantics=semantics or None, vmem_limit_bytes=grant * 2**20
+    )
 
 
 def wide(n):
@@ -240,7 +289,7 @@
             scratch_shapes=[pltpu.VMEM((ROWS, WIDTH_X), F32), pltpu.VMEM((128, WIDTH_X), BF16)],
         ),
         out_shape=jax.ShapeDtypeStruct((ROWS, width), BF16),
-        compiler_params=params(),
+        compiler_params=params(LAST, "arbitrary"),
         cost_estimate=pl.CostEstimate(flops=10**9, bytes_accessed=9 * 10**6, transcendentals=0),
     )(ids, part, act, scale, held, tabs)
 
@@ -256,27 +305,31 @@
     recv = lax.ppermute(xbc, "core", swap)
     dt_recv = lax.ppermute(dt_raw, "core", swap)
 
+    full = lambda *shape: pl.BlockSpec(shape, lambda i: (0,) * len(shape))
+    table, rim = pl.pallas_call(
+        table_kernel,
+        name="table",
+        grid=(1,),
+        in_specs=[
+            full(CONV, GROUP_W),
+            full(GROUP_W),
+            full(WIDTH_X),
+            full(PER_GROUP),
+            full(PER_GROUP),
+            pl.BlockSpec((16, GROUPS * GROUP_W), lambda i: (ROWS // 16 - 1, 0)),
+        ],
+        out_specs=[full(8, GROUP_W), full(LAG, GROUPS * GROUP_W)],
+        out_shape=[
+            jax.ShapeDtypeStruct((8, GROUP_W), F32),
+            jax.ShapeDtypeStruct((LAG, GROUPS * GROUP_W), BF16),
+        ],
+        compiler_params=params(SMALL, "arbitrary"),
+    )(conv_w, conv_b, gain, decay_rate, skip, xbc)
     names = ("x", "z", "y", "core")
-    rim = xbc[ROWS - LAG :]
     rims = [
         lax.ppermute(rim, names, [(2 * p + 1, 2 * p + 2 + k) for p in range(CHIPS - 1)])
         for k in range(2)
     ]
-
-    lanes = jnp.arange(128, dtype=jnp.int32) // PER_GROUP == y_at
-    small = jnp.concatenate(
-        [jnp.where(lanes, jnp.tile(decay_rate, 4), 0.0), jnp.where(lanes, jnp.tile(skip, 4), 0.0)]
-    )
-    table = jnp.concatenate(
-        [
-            conv_w.astype(F32),
-            conv_b.astype(F32)[None],
-            jnp.pad(gain.astype(F32), (0, GROUP_W - WIDTH_X))[None],
-            jnp.pad(small, (0, GROUP_W - 256))[None],
-            jnp.zeros((1, GROUP_W), F32),
-        ],
-        0,
-    )
     tables = [table] + [
         lax.ppermute(table, "y", [(i, (i + s) % 4) for i in range(4)]) for s in range(1, 4)
     ]
@@ -304,12 +357,12 @@
             ],
             scratch_shapes=[
                 pltpu.VMEM((GROUP_W // 128, 8 + CHUNK, 128), F32),
-                pltpu.VMEM((CHUNK, WIDTH_X), F32),
                 pltpu.VMEM((128, WIDTH_X), BF16),
                 pltpu.VMEM((CHUNK, 128), F32),
                 pltpu.VMEM((CHUNK, 128), F32),
                 pltpu.VMEM((8, 128), F32),
                 pltpu.VMEM((1, 256), F32),
+                pltpu.VMEM((CHUNK, 128), BF16),
             ],
         ),
         out_shape=[
@@ -320,7 +373,7 @@
             jax.ShapeDtypeStruct((LOC, CHUNK, 128), BF16),
             jax.ShapeDtypeStruct((LOC, 8, GROUP_W), F32),
         ],
-        compiler_params=params(),
+        compiler_params=params(FIRST, "arbitrary"),
         cost_estimate=pl.CostEstimate(flops=2 * 10**9, bytes_accessed=18 * 10**6, transcendentals=0),
     )(ids, starts, xbc, recv, *rims, dt_raw, dt_recv, *tables)
 
@@ -334,7 +387,7 @@
         out_specs=wide(WIDTH_X),
         out_shape=jax.ShapeDtypeStruct((CHUNK, LOC * WIDTH_X), F32),
         scratch_shapes=[pltpu.VMEM((128, WIDTH_X), BF16)],
-        compiler_params=params(),
+        compiler_params=params(INNER, "arbitrary"),
         cost_estimate=pl.CostEstimate(flops=2 * 10**9, bytes_accessed=20 * 10**6, transcendentals=0),
     )(score, xb, act, scale, tabs)
 
@@ -350,38 +403,44 @@
             jax.ShapeDtypeStruct((OWNERS, PAY, 128), BF16),
         ],
         scratch_shapes=[pltpu.VMEM((CHIPS, 128), F32)],
-        compiler_params=pltpu.CompilerParams(vmem_limit_bytes=24 * 2**20),
+        compiler_params=params(SCAN),
         cost_estimate=pl.CostEstimate(flops=10**7, bytes_accessed=5 * 10**6, transcendentals=0),
     )(ids, starts, assign, got)
 
     back = lax.all_to_all(held, ("y", "x", "z"), 0, 0, tiled=True)
-    back, fin = lax.optimization_barrier((back, fin))
     rows_got = lax.all_to_all(fin, ("x", "z"), 0, 0, tiled=True)
 
     back = back.reshape(LOC, OWNERS, STATE, 128)
     send = last_call(ids, part, act, scale, back, tabs, False)
     theirs = lax.ppermute(send, "core", swap)
     out = last_call(ids, part, act, scale, back, tabs, True)
+    hbm = pl.BlockSpec(memory_space=pl.ANY)
     mixed = pl.pallas_call(
         place_kernel,
         name="place",
-        grid_spec=pltpu.PrefetchScalarGridSpec(
-            num_scalar_prefetch=1,
-            grid=(LOC,),
-            in_specs=[
-                pl.BlockSpec(memory_space=pl.ANY),
-                pl.BlockSpec((ROWS, WIDTH_X), lambda g, ids: (0, g)),
-            ],
-            out_specs=pl.BlockSpec((ROWS, WIDTH_X), lambda g, ids: (0, 2 * g + 1 - ids[0])),
-        ),
+        in_specs=[smem, hbm, hbm],
+        out_specs=hbm,
         out_shape=jax.ShapeDtypeStruct((ROWS, GROUPS * WIDTH_X), BF16),
+        scratch_shapes=[
+            pltpu.VMEM((LOC, ROWS, WIDTH_X), BF16),
+            pltpu.SemaphoreType.DMA((LOC,)),
+            pltpu.SemaphoreType.DMA((LOC,)),
+        ],
         input_output_aliases={1: 0},
-        compiler_params=params(),
+        compiler_params=params(PLACE),
     )(ids, out, theirs)
-
-    states = rows_got[:, 0:STATE, :].astype(F32).reshape(1, PER_GROUP, HEAD_DIM, STATE)
-    tails = rows_got[:, STATE : STATE + 4, :].reshape(64, 128)[: LAG * GROUP_W // 128]
-    return (mixed, states, tails.reshape(1, LAG, GROUP_W))
+    states, tails = pl.pallas_call(
+        rows_kernel,
+        name="rows",
+        in_specs=[vmem],
+        out_specs=[vmem, vmem],
+        out_shape=[
+            jax.ShapeDtypeStruct((OWNERS, STATE, 128), F32),
+            jax.ShapeDtypeStruct((1, LAG, GROUP_W), BF16),
+        ],
+        compiler_params=params(EXTRA),
+    )(rows_got)
+    return (mixed, states.reshape(1, PER_GROUP, HEAD_DIM, STATE), tails)
 
 
 def solution(mesh):

time: 157 us -> 152 us (0.968)
  local copies, waits for them, and re-layouts: 33.1 us -> 0.89 us
  blocking collectives: 46.5 us -> 63.6 us
  Pallas kernels: 35.8 us -> 49.6 us
  starting transfers between devices: 17.7 us -> 13.7 us
  waiting for transfers between devices: 20.3 us -> 22.8 us
  other arithmetic: 1.8 us -> 0.01 us
    unnamed x28 -> x8, local copies, waits for them, and re-layouts: 26.6 us -> 0.89 us
    all_to_all x0 -> x1, blocking collectives: none -> 16.7 us  [shards(): rows_got = lax.all_to_all(fin, ('x', 'z'), 0, 0, tiled=True)]
    all_to_all x1 -> x0, starting transfers between devices: 4.25 us -> none  [shards(): rows_got = lax.all_to_all(fin, ('x', 'z'), 0, 0, tiled=True)]
    pallas_call x2, Pallas kernels: 8.91 us -> 12.9 us  [last_call(): pl.pallas_call(last_kernel, name='last', grid_spec=pltpu.PrefetchScalarGr...]
    all_to_all x1, waiting for transfers between devices: 17 us -> 21 us  [shards(): back = lax.all_to_all(held, ('y', 'x', 'z'), 0, 0, tiled=True)]
    pallas_call x1, Pallas kernels: 14.2 us -> 18 us  [shards(): pl.pallas_call(first_kernel, name='first', grid_spec=pltpu.PrefetchScalar...]
    pallas_call x1, Pallas kernels: 5.46 us -> 9.19 us  [shards(): pl.pallas_call(inner_kernel, name='inner', grid=(LOC,), in_specs=[wide(CH...]
    slice x4 -> x0, local copies, waits for them, and re-layouts: 2.88 us -> none  [the longest x1 1.08 us: shards(): rows_got[:, 0:STATE, :].astype(F32).reshape(1, PER_GROUP, HEAD_DIM, STATE)]
  transfers between devices with their start and end apart: 10 -> 9, of which waited for: 4 -> 4; matrix products, arithmetic and copies ran while one was open for 5% -> 0% of each run, Pallas kernels for 6% -> 12%
where the time goes in v3:
time: 152 us; the launch traced here: 151 us
  blocking collectives  63.6 us (42%)
  Pallas kernels  49.6 us (33%)
  waiting for transfers between devices  22.8 us (15%)
  starting transfers between devices  13.7 us (9%)
    all_to_all x1, blocking collectives, shards(): lax.all_to_all(pay.reshape(CHIPS, PAY, 128), ('y', 'x', 'z'), 0, 0, tiled...  46.9 us
    all_to_all x1, waiting for transfers between devices, shards(): back = lax.all_to_all(held, ('y', 'x', 'z'), 0, 0, tiled=True)  21 us
    pallas_call x1, Pallas kernels, shards(): pl.pallas_call(first_kernel, name='first', grid_spec=pltpu.PrefetchScalar...  18 us
    all_to_all x1, blocking collectives, shards(): rows_got = lax.all_to_all(fin, ('x', 'z'), 0, 0, tiled=True)  16.7 us
    pallas_call x2, Pallas kernels, last_call(): pl.pallas_call(last_kernel, name='last', grid_spec=pltpu.PrefetchScalarGr...  12.9 us
    pallas_call x1, Pallas kernels, shards(): pl.pallas_call(inner_kernel, name='inner', grid=(LOC,), in_specs=[wide(CH...  9.19 us
    all_to_all x1, starting transfers between devices, shards(): back = lax.all_to_all(held, ('y', 'x', 'z'), 0, 0, tiled=True)  6.14 us
    ppermute x3, starting transfers between devices, shards(): lax.ppermute(table, 'y', [(i, (i + s) % 4) for i in range(4)])  5.94 us
  transfers between devices with their start and end apart: 9, of which 4 were waited for; matrix products, arithmetic and copies ran while one was open for 0% of the time, Pallas kernels for 12%

profile of v3, /device:TPU:0, one launch (start us, length us, event | category | flops | bytes accessed | tf_op | source)
XLA Modules:
  0.0 151.4 jit_solution(15574861197197407544)
XLA Ops:
  0.6 0.0 copy-start.1
  0.6 0.0 copy-start.2
  0.7 0.1 collective-permute-start
  0.7 1.9 %table.1 = (f32[8,2304]{1,0:T(8,128)}, bf16[3,18432]{1,0:T(4,128)(2,1)}) custom-call(bf16[4,2304]{1,0:T(4,128)(2,1)} %conv_w.1, bf16[2304]{0:T(1024)(128)(2,1)} %conv_b.1, bf16[2048]{0:T(1024)(128)(2,1)} %gain.1, f32[32]{0:T(128)} %decay.1, f32[32]{0:T(128)} %skip.1, bf16[128,18432]{1,0:T(8,128)(2,1)} %mine.1), custom_call_target="tpu_custom_call" | custom-call | tf_op jit(solution)/shard_map/table/pallas_call | solution.py:309
  2.7 1.7 %collective-permute-start.4 = (f32[8,2304]{1,0:T(8,128)}, f32[8,2304]{1,0:T(8,128)S(1)}, u32[]{:S(2)}, u32[]{:S(2)}) collective-permute-start(f32[8,2304]{1,0:T(8,128)} %get-tuple-element.16.tab0), channel_id=1, source_target_pairs={{0,2},{2,4},{4,6},{6,0},{1,3},{3,5},{5,7},{7,1},{8,10},{10,12},{12... | collective-permute-start | bytes 221192 | tf_op jit(solution)/shard_map/ppermute | solution.py:334
  4.4 0.0 copy-done.1
  4.4 0.2 collective-permute-start.3
  4.6 2.9 %collective-permute-start.5 = (f32[8,2304]{1,0:T(8,128)}, f32[8,2304]{1,0:T(8,128)S(1)}, u32[]{:S(2)}, u32[]{:S(2)}) collective-permute-start(f32[8,2304]{1,0:T(8,128)} %get-tuple-element.16.tab0), channel_id=1, source_target_pairs={{0,4},{2,6},{4,0},{6,2},{1,5},{3,7},{5,1},{7,3},{8,12},{10,14},{12... | collective-permute-start | bytes 221192 | tf_op jit(solution)/shard_map/ppermute | solution.py:334
  7.5 1.3 collective-permute-start.6
  8.8 0.2 collective-permute-done.3.dt_recv
  9.0 0.7 collective-permute-start.1
  9.7 0.0 collective-permute-done.4.tab1
  9.7 0.7 collective-permute-start.2
  10.4 1.3 collective-permute-done.5.tab2
  11.7 0.3 collective-permute-done.6.tab3
  12.0 0.0 collective-permute-done.1.rim_a
  12.0 0.0 collective-permute-done.2.rim_b
  12.0 0.0 collective-permute-done.recv
  12.0 0.0 copy-done.2
  12.1 0.0 copy-start
  12.1 0.9 copy-done
  12.9 18.0 %first.1 = (bf16[4,16,136,128]{3,2,1,0:T(8,128)(2,1)}, bf16[256,9216]{1,0:T(8,128)(2,1)}, bf16[256,8192]{1,0:T(8,128)(2,1)}, bf16[256,1024]{1,0:T(8,128)(2,1)S(1...) custom-call(s32[4]{0:T(128)S(1)} %compare_select_fusion.1.ids, s32[16]{0:T(128)S(1)} %copy-done.2, ...), custom_call_target="tpu_custom_call" | custom-call | flops 2000000000 | bytes 18000000 | tf_op jit(solution)/shard_map/first/pallas_call | solution.py:343
  30.9 0.0 copy-start.3
  30.9 46.9 %all_to_all.15.got = bf16[64,136,128]{2,1,0:T(8,128)(2,1)} all-to-all(bf16[64,136,128]{2,1,0:T(8,128)(2,1)} %bitcast.3), channel_id=1, replica_groups=mesh['x'=4,'z'=4,'y'=4,'core'=2] {'y','x','z'}, dimensions={0} | all-to-all | bytes 4456448 | tf_op jit(solution)/shard_map/all_to_all | solution.py:380
  77.9 0.0 copy-done.3
  77.9 4.4 %scan.1 = (bf16[64,128,128]{2,1,0:T(8,128)(2,1)}, bf16[16,136,128]{2,1,0:T(8,128)(2,1)S(1)}) custom-call(s32[4]{0:T(128)S(1)} %compare_select_fusion.1.ids, s32[16]{0:T(128)S(1)} %copy-done.2, s32[4]{0:T(128)S(1)} %copy-done.3, bf16[64,136,128]{2,1,0:T(8,128)(2,1)} %all_to_all.15.got), custom_call_target="tpu_custom_call" | custom-call | flops 10000000 | bytes 5000000 | tf_op jit(solution)/shard_map/scan/pallas_call | solution.py:396
  82.3 6.1 %all-to-all-start.1 = ((bf16[64,128,128]{2,1,0:T(8,128)(2,1)}), bf16[64,128,128]{2,1,0:T(8,128)(2,1)}, u32[]{:S(2)}, u32[]{:S(2)}) async-start(bf16[64,128,128]{2,1,0:T(8,128)(2,1)} %get-tuple-element.23), calls=%async_computation.1 | async-start | bytes 4194304 | tf_op jit(solution)/shard_map/all_to_all | solution.py:410
  88.5 9.2 %inner.1.part = f32[256,8192]{1,0:T(8,128)} custom-call(bf16[256,1024]{1,0:T(8,128)(2,1)S(1)} %get-tuple-element.17.score, bf16[256,8192]{1,0:T(8,128)(2,1)} %get-tuple-element.18.xb, bf16[256,9216]{1,0:T(8,128)(2,1)} %get-tuple-element.19.act.act_c, bf16[4,256,128]{2,1,0:T(8,128)(2,1)S(1)} %get-tuple-element.20.scale, f32[4,8,2304]{2,1,0:T(8,128)S(1)} %get-tuple-element.21.tabs), custom_call_target="tpu_custom_call" | custom-call | flops 2000000000 | bytes 20000000 | tf_op jit(solution)/shard_map/inner/pallas_call | solution.py:382
  97.7 21.0 %all-to-all-done.1 = bf16[64,128,128]{2,1,0:T(8,128)(2,1)} async-done(((bf16[64,128,128]{2,1,0:T(8,128)(2,1)}), bf16[64,128,128]{2,1,0:T(8,128)(2,1)}, u32[]{:S(2)}, u32[]{:S(2)}) %all-to-all-start.1) | async-done | bytes 2097184 | tf_op jit(solution)/shard_map/all_to_all | solution.py:410
  118.6 6.5 %last.3 = bf16[128,8192]{1,0:T(8,128)(2,1)} custom-call(s32[4]{0:T(128)S(1)} %compare_select_fusion.1.ids, f32[256,8192]{1,0:T(8,128)} %inner.1.part, bf16[256,9216]{1,0:T(8,128)(2,1)} %get-tuple-element.19.act.act_c, bf16[4,256,128]{2,1,0:T(8,128)(2,1)S(1)} %get-tuple-element.20.scale, bf16[4,16,128,128]{3,2,1,0:T(8,128)(2,1)} %bitcast.1.held, ...), custom_call_target="tpu_custom_call" | custom-call | flops 1000000000 | bytes 9000000 | tf_op jit(solution)/shard_map/last/pallas_call | solution.py:275
  125.1 0.0 collective-permute-start.7
  125.1 16.7 %all_to_all.16.got = bf16[16,136,128]{2,1,0:T(8,128)(2,1)S(1)} all-to-all(bf16[16,136,128]{2,1,0:T(8,128)(2,1)S(1)} %get-tuple-element.24), channel_id=1, replica_groups=mesh['x'=4,'z'=4,'y'=4,'core'=2] {'x','z'}, dimensions={0} | all-to-all | bytes 1114112 | tf_op jit(solution)/shard_map/all_to_all | solution.py:411
  141.8 1.1 rows.3
  142.8 6.4 %last.2.whole = bf16[128,16384]{1,0:T(8,128)(2,1)} custom-call(s32[4]{0:T(128)S(1)} %compare_select_fusion.1.ids, f32[256,8192]{1,0:T(8,128)} %inner.1.part, bf16[256,9216]{1,0:T(8,128)(2,1)} %get-tuple-element.19.act.act_c, bf16[4,256,128]{2,1,0:T(8,128)(2,1)S(1)} %get-tuple-element.20.scale, bf16[4,16,128,128]{3,2,1,0:T(8,128)(2,1)} %bitcast.1.held, ...), custom_call_target="tpu_custom_call" | custom-call | flops 1000000000 | bytes 9000000 | tf_op jit(solution)/shard_map/last/pallas_call | solution.py:275
  149.3 0.0 collective-permute-done.7.theirs
  149.3 2.1 %place.1 = bf16[128,16384]{1,0:T(8,128)(2,1)} custom-call(s32[4]{0:T(128)S(1)} %compare_select_fusion.1.ids, bf16[128,16384]{1,0:T(8,128)(2,1)} %last.2.whole, bf16[128,8192]{1,0:T(8,128)(2,1)S(1)} %collective-permute-done.7.theirs), custom_call_target="tpu_custom_call", output_to_operand_aliasing={{}: (1, {})} | custom-call | tf_op jit(solution)/shard_map/place/pallas_call | solution.py:418
  (1 shorter events, 0.0 us)
Async XLA Ops:
  0.6 3.7 %copy-start.1 = (bf16[128,256]{1,0:T(8,128)(2,1)S(1)}, bf16[128,256]{1,0:T(8,128)(2,1)}, u32[]{:S(2)}) copy-start(bf16[128,256]{1,0:T(8,128)(2,1)} %dt_mine.1) | copy-start | bytes 196612
  0.6 11.4 %copy-start.2 = (s32[16]{0:T(128)S(1)}, s32[16]{0:T(128)}, u32[]{:S(2)}) copy-start(s32[16]{0:T(128)} %starts.3) | copy-start | bytes 196
  0.7 11.4 %collective-permute-start = (bf16[128,18432]{1,0:T(8,128)(2,1)}, bf16[128,18432]{1,0:T(8,128)(2,1)}, u32[]{:S(2)}, u32[]{:S(2)}) collective-permute-start(bf16[128,18432]{1,0:T(8,128)(2,1)} %mine.1), channel_id=1, source_target_pairs={{0,1},{1,0},{2,3},{3,2},{4,5},{5,4},{6,7},{7,6},{8,9},{9,8},{10,11... | collective-permute-start | bytes 14155784 | tf_op jit(solution)/shard_map/ppermute | solution.py:305
  2.7 7.0 %collective-permute-start.4 = (f32[8,2304]{1,0:T(8,128)}, f32[8,2304]{1,0:T(8,128)S(1)}, u32[]{:S(2)}, u32[]{:S(2)}) collective-permute-start(f32[8,2304]{1,0:T(8,128)} %get-tuple-element.16.tab0), channel_id=1, source_target_pairs={{0,2},{2,4},{4,6},{6,0},{1,3},{3,5},{5,7},{7,1},{8,10},{10,12},{12... | collective-permute-start | bytes 221192 | tf_op jit(solution)/shard_map/ppermute | solution.py:334
  4.4 4.6 %collective-permute-start.3 = (bf16[128,256]{1,0:T(8,128)(2,1)S(1)}, bf16[128,256]{1,0:T(8,128)(2,1)S(1)}, u32[]{:S(2)}, u32[]{:S(2)}) collective-permute-start(bf16[128,256]{1,0:T(8,128)(2,1)S(1)} %copy-done.1), channel_id=1, source_target_pairs={{0,1},{1,0},{2,3},{3,2},{4,5},{5,4},{6,7},{7,6},{8,9},{9,8},{10,11... | collective-permute-start | bytes 196616 | tf_op jit(solution)/shard_map/ppermute | solution.py:306
  4.6 7.1 %collective-permute-start.5 = (f32[8,2304]{1,0:T(8,128)}, f32[8,2304]{1,0:T(8,128)S(1)}, u32[]{:S(2)}, u32[]{:S(2)}) collective-permute-start(f32[8,2304]{1,0:T(8,128)} %get-tuple-element.16.tab0), channel_id=1, source_target_pairs={{0,4},{2,6},{4,0},{6,2},{1,5},{3,7},{5,1},{7,3},{8,12},{10,14},{12... | collective-permute-start | bytes 221192 | tf_op jit(solution)/shard_map/ppermute | solution.py:334
  7.5 4.6 %collective-permute-start.6 = (f32[8,2304]{1,0:T(8,128)}, f32[8,2304]{1,0:T(8,128)S(1)}, u32[]{:S(2)}, u32[]{:S(2)}) collective-permute-start(f32[8,2304]{1,0:T(8,128)} %get-tuple-element.16.tab0), channel_id=1, source_target_pairs={{0,6},{2,0},{4,2},{6,4},{1,7},{3,1},{5,3},{7,5},{8,14},{10,8},{12,... | collective-permute-start | bytes 221192 | tf_op jit(solution)/shard_map/ppermute | solution.py:334
  9.0 3.0 %collective-permute-start.1 = (bf16[3,18432]{1,0:T(4,128)(2,1)}, bf16[3,18432]{1,0:T(4,128)(2,1)S(1)}, u32[]{:S(2)}, u32[]{:S(2)}) collective-permute-start(bf16[3,18432]{1,0:T(4,128)(2,1)} %get-tuple-element.15), channel_id=1, source_target_pairs={{1,2},{3,4},{5,6},{7,8},{9,10},{11,12},{13,14},{15,16},{17,18},{19... | collective-permute-start | bytes 331784 | tf_op jit(solution)/shard_map/ppermute | solution.py:330
  9.7 2.4 %collective-permute-start.2 = (bf16[3,18432]{1,0:T(4,128)(2,1)}, bf16[3,18432]{1,0:T(4,128)(2,1)S(1)}, u32[]{:S(2)}, u32[]{:S(2)}) collective-permute-start(bf16[3,18432]{1,0:T(4,128)(2,1)} %get-tuple-element.15), channel_id=1, source_target_pairs={{1,3},{3,5},{5,7},{7,9},{9,11},{11,13},{13,15},{15,17},{17,19},{19... | collective-permute-start | bytes 331784 | tf_op jit(solution)/shard_map/ppermute | solution.py:330
  12.1 0.9 copy-start
  30.9 46.9 %copy-start.3 = (s32[4]{0:T(128)S(1)}, s32[4]{0:T(128)}, u32[]{:S(2)}) copy-start(s32[4]{0:T(128)} %assign.1) | copy-start | bytes 52
  82.3 36.3 %all-to-all-start.1 = ((bf16[64,128,128]{2,1,0:T(8,128)(2,1)}), bf16[64,128,128]{2,1,0:T(8,128)(2,1)}, u32[]{:S(2)}, u32[]{:S(2)}) async-start(bf16[64,128,128]{2,1,0:T(8,128)(2,1)} %get-tuple-element.23), calls=%async_computation.1 | async-start | bytes 4194304 | tf_op jit(solution)/shard_map/all_to_all | solution.py:410
  125.1 24.2 %collective-permute-start.7 = (bf16[128,8192]{1,0:T(8,128)(2,1)}, bf16[128,8192]{1,0:T(8,128)(2,1)S(1)}, u32[]{:S(2)}, u32[]{:S(2)}) collective-permute-start(bf16[128,8192]{1,0:T(8,128)(2,1)} %last.3), channel_id=1, source_target_pairs={{0,1},{1,0},{2,3},{3,2},{4,5},{5,4},{6,7},{7,6},{8,9},{9,8},{10,11... | collective-permute-start | bytes 6291464 | tf_op jit(solution)/shard_map/ppermute | solution.py:415

commit v4 on v3

v4 whole, which is shorter than its diff:
```python
import functools

import jax
import jax.numpy as jnp
from jax import lax
from jax.experimental import pallas as pl
from jax.experimental.pallas import tpu as pltpu
from jax.sharding import Mesh, PartitionSpec as P


HEAD_DIM = 64
STATE = 128
GROUPS = 8
PER_GROUP = 32
WIDTH_X = PER_GROUP * HEAD_DIM
GROUP_W = WIDTH_X + 2 * STATE
LOC = GROUPS // 2
ROWS = 128
CHUNK = 2 * ROWS
CHIPS = 64
OWNERS = 16
PAY = 136
CONV = 4
LAG = CONV - 1

F32 = jnp.float32
BF16 = jnp.bfloat16


def dot(a, b, ca=1, cb=0):
    return lax.dot_general(a, b, (((ca,), (cb,)), ((), ())), preferred_element_type=F32)


def halves(v):
    hi = v.astype(BF16).astype(F32)
    return hi, (v - hi).astype(BF16).astype(F32)


def pack(hi, low, g):
    lane = lax.broadcasted_iota(jnp.int32, hi.shape, 1)
    both = jnp.where(
        lane < 32, pltpu.roll(hi, (128 - g * PER_GROUP) & 127, 1), pltpu.roll(low, (160 - g * PER_GROUP) & 127, 1)
    )
    return jnp.where(lane < 64, both, 0.0).astype(BF16)


def spread():
    row = lax.broadcasted_iota(jnp.int32, (128, WIDTH_X), 0)
    col = lax.broadcasted_iota(jnp.int32, (128, WIDTH_X), 1)
    return ((row & 31) == (col >> 6)).astype(F32).astype(BF16)


def table_kernel(conv_w, conv_b, gain, decay, skip, rows, table, rim):
    table[0:CONV] = 0.5 * conv_w[...].astype(F32)
    table[CONV : CONV + 1] = 0.5 * conv_b[...].astype(F32).reshape(1, GROUP_W)
    table[CONV + 1 : CONV + 2, 0:WIDTH_X] = gain[...].astype(F32).reshape(1, WIDTH_X)
    table[CONV + 1 : CONV + 2, WIDTH_X:] = jnp.zeros((1, GROUP_W - WIDTH_X), F32)
    table[CONV + 2 :] = jnp.zeros((8 - CONV - 2, GROUP_W), F32)
    d, s = decay[...].reshape(1, PER_GROUP), skip[...].reshape(1, PER_GROUP)
    table[CONV + 2 : CONV + 3, 0:256] = jnp.concatenate([d] * 4 + [s] * 4, 1)
    rim[...] = rows[...].astype(F32)[16 - LAG :].astype(BF16)


def first_kernel(ids, starts, mine, recv, rim_a, rim_b, dt_mine, dt_recv, tab0, tab1, tab2, tab3,
                 pay, act, scale, tabs, xb, ext_a, ext_b, one_hot, full, lrow, small, even, odd, ends):
    g = pl.program_id(0)
    core = ids[0]
    own = pl.multiple_of(core * ROWS, ROWS)
    other = pl.multiple_of((1 - core) * ROWS, ROWS)

    @pl.when(g == 0)
    def _():
        col = lax.broadcasted_iota(jnp.int32, (2 * 128, 128), 0)
        lane = lax.broadcasted_iota(jnp.int32, (2 * 128, 128), 1)
        pick = (col == ((2 * (lane >> 5) + core) << 5) + (lane & 31)).astype(F32).astype(BF16)
        full[0, pl.ds(own, ROWS), :] = dot(dt_mine[...], pick)
        full[0, pl.ds(other, ROWS), :] = dot(dt_recv[...], pick)
        step = jnp.log1p(jnp.exp(full[0]))
        block = (lax.broadcasted_iota(jnp.int32, (1, 256), 1) >> 5) & 3
        every = jnp.zeros((1, 256), F32)
        for shift, tab in enumerate((tab0, tab1, tab2, tab3)):
            every = every + jnp.where(block == ((ids[1] - shift) & 3), tab[6:7, 0:256], 0.0)
        small[...] = every
        cum = -step * every[:, 0:128]
        row = lax.broadcasted_iota(jnp.int32, (CHUNK, 128), 0)
        shift = 1
        while shift < CHUNK:
            cum = cum + jnp.where(row >= shift, pltpu.roll(cum, shift, 0), 0.0)
            shift *= 2
        full[0], full[1] = halves(jnp.exp(cum))
        full[2], full[3] = halves(jnp.exp(-cum) * step)
        last = cum[CHUNK - 8 :, :]
        hi, rest = halves(last)
        low = (last - hi - rest).astype(BF16).astype(F32)
        lrow[0:1] = hi[7:8]
        lrow[1:2] = rest[7:8]
        lrow[2:3] = low[7:8]
        lrow[3:8] = jnp.zeros((5, 128), F32)
        one_hot[...] = spread()

    shift = (ids[1] - g) & 3
    table = jnp.where(
        shift == 0, tab0[...], jnp.where(shift == 1, tab1[...], jnp.where(shift == 2, tab2[...], tab3[...]))
    )
    tabs[0] = table
    tabs[0, 7:8, 0:256] = small[...]
    scale[0, 0] = pack(full[0], full[1], g)
    scale[0, 1] = pack(full[2], full[3], g)
    opens = starts[ids[2]] == ids[1] * CHUNK

    def columns(j):
        return pl.ds(j * 128 if isinstance(j, int) else pl.multiple_of(j * 128, 128), 128)

    def conv(j, ext):
        at = columns(j)
        halo = rim_a[:, at].astype(F32) + rim_b[:, at].astype(F32)
        ext[8 - LAG : 8, :] = jnp.where(opens, jnp.zeros_like(halo), halo)
        ext[pl.ds(8 + own, ROWS), :] = mine[:, at].astype(F32)
        ext[pl.ds(8 + other, ROWS), :] = recv[:, at].astype(F32)
        half = tabs[0, CONV : CONV + 1, at] + ext[8 - LAG : 8 - LAG + CHUNK, :] * tabs[0, 0:1, at]
        for tap in range(1, CONV):
            half = half + ext[8 - LAG + tap : 8 - LAG + tap + CHUNK, :] * tabs[0, tap : tap + 1, at]
        ends[j] = ext[CHUNK : CHUNK + 8, :]
        val = (half * jnp.tanh(half) + half).astype(BF16)
        act[:, at] = val
        return val

    strips = WIDTH_X // 128
    b_in = conv(strips, ext_a)
    conv(strips + 1, ext_b)
    b_t = b_in.astype(F32).T.astype(BF16)

    def weights(j):
        return dot(scale[0, 1], one_hot[:, columns(j)])

    def fresh(j):
        pay[0, j, 0:STATE, :] = dot(b_t, xb[:, columns(j)]).astype(BF16)

    def weigh(j, ext, factor):
        xb[:, columns(j)] = (conv(j, ext).astype(F32) * factor[...]).astype(BF16)

    def pair(i, behind):
        if behind:
            fresh(2 * i - 2)
            fresh(2 * i - 1)
        odd[...] = weights(2 * i + 1)
        weigh(2 * i, ext_a, even)
        even[...] = weights((2 * i + 2) & (strips - 1))
        weigh(2 * i + 1, ext_b, odd)

    even[...] = weights(0)
    pair(0, False)

    def trip(i, _):
        pair(i, True)
        return 0

    lax.fori_loop(1, strips // 2, trip, 0)
    fresh(strips - 2)
    fresh(strips - 1)
    for o in range(OWNERS):
        rows = []
        for slot in range(4):
            tap, block = divmod(o * 4 + slot, GROUP_W // 128)
            if tap < LAG:
                rows.append(ends[block, 8 - LAG + tap : 9 - LAG + tap, :])
            else:
                rows.append(jnp.zeros((1, 128), F32))
        pay[0, o, STATE:PAY, :] = jnp.concatenate(rows + [lrow[0:4]], 0).astype(BF16)


def inner_kernel(act, scale, tabs, part, one_hot):
    g = pl.program_id(0)

    @pl.when(g == 0)
    def _():
        one_hot[...] = spread()

    skip_hi, rest = halves(jnp.broadcast_to(tabs[0, 7:8, 128:256], (8, 128)))
    skip = pack(skip_hi, rest, g)
    s = dot(act[:, WIDTH_X + STATE :], act[:, WIDTH_X : WIDTH_X + STATE], 1, 1)
    t_at = lax.broadcasted_iota(jnp.int32, (CHUNK, CHUNK), 0)
    s_at = lax.broadcasted_iota(jnp.int32, (CHUNK, CHUNK), 1)
    s = jnp.where(s_at <= t_at, s, 0.0).astype(BF16)
    for j in range(0, WIDTH_X, 256):
        at = slice(j, j + 256)
        e = one_hot[:, at]
        x = act[:, at].astype(F32)
        xb = (x * dot(scale[0, 1], e)).astype(BF16)
        part[:, at] = dot(scale[0, 0], e) * dot(s, xb) + dot(skip, e)[0:1] * x


def scan_kernel(ids, starts, assign, got, held, fin, dec, after):
    lane = lax.broadcasted_iota(jnp.int32, (CHIPS, 128), 1)
    total = (got[:, STATE + 4, :].astype(F32) + got[:, STATE + 5, :].astype(F32)
             + got[:, STATE + 6, :].astype(F32))
    head = ids[1] * PER_GROUP + ids[2] * 2
    d0 = jnp.sum(jnp.where(lane == head, total, 0.0), 1, keepdims=True)
    d1 = jnp.sum(jnp.where(lane == head + 1, total, 0.0), 1, keepdims=True)
    dec[...] = jnp.exp(jnp.where(lane < HEAD_DIM, d0, d1))
    fin[...] = jnp.zeros_like(fin)

    def step(ctx, state):
        for y in range(4):
            at = y * OWNERS + ctx
            if y % 2 == 0:
                state = jnp.where(starts[ctx] == y * CHUNK, 0.0, state)
            held[at] = state.astype(BF16)
            state = dec[pl.ds(at, 1), :] * (state + got[at, 0:STATE, :].astype(F32))
            if y % 2:
                after[2 * ctx + y // 2] = state
        return state

    lax.fori_loop(0, OWNERS, step, jnp.zeros((STATE, 128), F32))

    def close(i, count):
        ctx, second = i >> 1, i & 1
        count = count + (starts[ctx] == second * 2 * CHUNK).astype(jnp.int32)
        follow = starts[jnp.minimum(ctx + 1, OWNERS - 1)]
        ends = jnp.where(second == 1, (ctx == OWNERS - 1) | (follow == 0), starts[ctx] == 2 * CHUNK)

        @pl.when(ends)
        def _():
            to = assign[count - 1]
            fin[to, 0:STATE, :] = after[i].T.astype(BF16)
            fin[to, STATE:PAY, :] = got[(2 * second + 1) * OWNERS + ctx, STATE:PAY, :]

        return count

    lax.fori_loop(0, 2 * OWNERS, close, jnp.int32(0))


def last_kernel(row_at, col_at, ids, part, act, scale, held, tabs, out,
                y, one_hot, part_in, c_in, scale_in, held_in, tab_in, done, sem_in, sem_out):
    rows = pl.ds(pl.multiple_of(row_at(ids) * ROWS, ROWS), ROWS)
    loads = []
    for g in range(LOC):
        wide_cols = pl.ds(g * WIDTH_X, WIDTH_X)
        c_cols = pl.ds((g + 1) * GROUP_W - STATE, STATE)
        loads.append([
            pltpu.make_async_copy(held.at[g], held_in.at[g], sem_in.at[g, 0]),
            pltpu.make_async_copy(act.at[rows, c_cols], c_in.at[g], sem_in.at[g, 1]),
            pltpu.make_async_copy(scale.at[g, 0, rows], scale_in.at[g], sem_in.at[g, 2]),
            pltpu.make_async_copy(part.at[rows, wide_cols], part_in.at[g], sem_in.at[g, 3]),
            pltpu.make_async_copy(tabs.at[g], tab_in.at[g], sem_in.at[g, 4]),
        ])
    for group in loads:
        for copy in group:
            copy.start()
    one_hot[...] = spread()
    stores = []
    for g in range(LOC):
        for copy in loads[g]:
            copy.wait()
        c = c_in[g]
        square = jnp.zeros((ROWS, 128), F32)
        for o in range(0, OWNERS, 2):
            at = slice(o * 128, (o + 2) * 128)
            h = jnp.concatenate([held_in[g, o], held_in[g, o + 1]], 1)
            total = part_in[g, :, at] + dot(scale_in[g], one_hot[:, at]) * dot(c, h)
            y[:, at] = total
            square = square + total[:, :128] * total[:, :128] + total[:, 128:] * total[:, 128:]
        mean = jnp.sum(square, 1, keepdims=True) * (1.0 / WIDTH_X)
        inv = jnp.broadcast_to(lax.rsqrt(mean + 1e-05), (ROWS, 128))
        for j in range(0, WIDTH_X, 128):
            at = slice(j, j + 128)
            done[g, :, at] = (y[:, at] * inv * tab_in[g, CONV + 1 : CONV + 2, at]).astype(BF16)
        to = pl.ds(pl.multiple_of(col_at(g, ids) * WIDTH_X, WIDTH_X), WIDTH_X)
        stores.append(pltpu.make_async_copy(done.at[g], out.at[:, to], sem_out.at[g]))
        stores[g].start()
    for store in stores:
        store.wait()


def place_kernel(ids, whole, theirs, out, held, sem_in, sem_out):
    def loads(g):
        cols = pl.ds(g * WIDTH_X, WIDTH_X)
        return pltpu.make_async_copy(theirs.at[:, cols], held.at[g], sem_in.at[g])

    def stores(g):
        cols = pl.ds(pl.multiple_of((2 * g + 1 - ids[0]) * WIDTH_X, WIDTH_X), WIDTH_X)
        return pltpu.make_async_copy(held.at[g], out.at[:, cols], sem_out.at[g])

    for g in range(LOC):
        loads(g).start()
    for g in range(LOC):
        loads(g).wait()
        stores(g).start()
    for g in range(LOC):
        stores(g).wait()


def rows_kernel(got, states, tails):
    states[...] = got[:, 0:STATE, :].astype(F32)
    for piece in range(LAG * GROUP_W // 128):
        tap, block = divmod(piece, GROUP_W // 128)
        row = STATE + piece % 4
        tails[0, tap : tap + 1, block * 128 : (block + 1) * 128] = got[piece // 4, row : row + 1, :]


FIRST, INNER, SCAN, LAST, PLACE, EXTRA, SMALL = 52, 52, 40, 52, 44, 52, 60


def params(grant, *semantics):
    return pltpu.CompilerParams(
        dimension_semantics=semantics or None, vmem_limit_bytes=grant * 2**20
    )


def wide(n):
    return pl.BlockSpec((CHUNK, n), lambda g, *_: (0, g))


TABLE = pl.BlockSpec((1, 8, GROUP_W), lambda g, *_: (g, 0, 0))


SMEM = pl.BlockSpec(memory_space=pltpu.SMEM)
VMEM = pl.BlockSpec(memory_space=pltpu.VMEM)
HBM = pl.BlockSpec(memory_space=pl.ANY)


def last_call(ids, part, act, scale, held, tabs, own):
    row_at = (lambda ids: ids[0]) if own else (lambda ids: 1 - ids[0])
    col_at = (lambda g, ids: 2 * g + ids[0]) if own else (lambda g, ids: g)
    width = (GROUPS if own else LOC) * WIDTH_X
    return pl.pallas_call(
        functools.partial(last_kernel, row_at, col_at),
        name="last",
        in_specs=[SMEM] + [HBM] * 5,
        out_specs=HBM,
        out_shape=jax.ShapeDtypeStruct((ROWS, width), BF16),
        scratch_shapes=[
            pltpu.VMEM((ROWS, WIDTH_X), F32),
            pltpu.VMEM((128, WIDTH_X), BF16),
            pltpu.VMEM((LOC, ROWS, WIDTH_X), F32),
            pltpu.VMEM((LOC, ROWS, STATE), BF16),
            pltpu.VMEM((LOC, ROWS, 128), BF16),
            pltpu.VMEM((LOC, OWNERS, STATE, 128), BF16),
            pltpu.VMEM((LOC, 8, GROUP_W), F32),
            pltpu.VMEM((LOC, ROWS, WIDTH_X), BF16),
            pltpu.SemaphoreType.DMA((LOC, 5)),
            pltpu.SemaphoreType.DMA((LOC,)),
        ],
        compiler_params=params(LAST),
        cost_estimate=pl.CostEstimate(flops=10**9, bytes_accessed=9 * 10**6, transcendentals=0),
    )(ids, part, act, scale, held, tabs)


def shards(xbc, dt_raw, decay_rate, skip, conv_w, conv_b, gain, starts, assign):
    core = lax.axis_index("core").astype(jnp.int32)
    y_at = lax.axis_index("y").astype(jnp.int32)
    ctx = (lax.axis_index("x") * 4 + lax.axis_index("z")).astype(jnp.int32)
    at = jnp.arange(4, dtype=jnp.int32)
    ids = jnp.where(at == 0, core, jnp.where(at == 1, y_at, ctx))

    swap = [(0, 1), (1, 0)]
    recv = lax.ppermute(xbc, "core", swap)
    dt_recv = lax.ppermute(dt_raw, "core", swap)

    full = lambda *shape: pl.BlockSpec(shape, lambda i: (0,) * len(shape))
    table, rim = pl.pallas_call(
        table_kernel,
        name="table",
        grid=(1,),
        in_specs=[
            full(CONV, GROUP_W),
            full(GROUP_W),
            full(WIDTH_X),
            full(PER_GROUP),
            full(PER_GROUP),
            pl.BlockSpec((16, GROUPS * GROUP_W), lambda i: (ROWS // 16 - 1, 0)),
        ],
        out_specs=[full(8, GROUP_W), full(LAG, GROUPS * GROUP_W)],
        out_shape=[
            jax.ShapeDtypeStruct((8, GROUP_W), F32),
            jax.ShapeDtypeStruct((LAG, GROUPS * GROUP_W), BF16),
        ],
        compiler_params=params(SMALL, "arbitrary"),
    )(conv_w, conv_b, gain, decay_rate, skip, xbc)
    names = ("x", "z", "y", "core")
    rims = [
        lax.ppermute(rim, names, [(2 * p + 1, 2 * p + 2 + k) for p in range(CHIPS - 1)])
        for k in range(2)
    ]
    tables = [table] + [
        lax.ppermute(table, "y", [(i, (i + s) % 4) for i in range(4)]) for s in range(1, 4)
    ]

    whole_table = pl.BlockSpec((8, GROUP_W), lambda g, *_: (0, 0))
    rows_spec = pl.BlockSpec((ROWS, GROUP_W), lambda g, ids, st: (0, 2 * g + ids[0]))
    rim_spec = pl.BlockSpec((LAG, GROUP_W), lambda g, ids, st: (0, 2 * g + ids[0]))
    dt_spec = pl.BlockSpec((ROWS, 256), lambda g, ids, st: (0, 0))
    scale_spec = pl.BlockSpec((1, 2, CHUNK, 128), lambda g, *_: (g, 0, 0, 0))

    pay, act, scale, tabs = pl.pallas_call(
        first_kernel,
        name="first",
        grid_spec=pltpu.PrefetchScalarGridSpec(
            num_scalar_prefetch=2,
            grid=(LOC,),
            in_specs=[rows_spec] * 2 + [rim_spec] * 2 + [dt_spec] * 2 + [whole_table] * 4,
            out_specs=[
                pl.BlockSpec((1, OWNERS, PAY, 128), lambda g, *_: (g, 0, 0, 0)),
                wide(GROUP_W),
                scale_spec,
                TABLE,
            ],
            scratch_shapes=[
                pltpu.VMEM((CHUNK, WIDTH_X), BF16),
                pltpu.VMEM((8 + CHUNK, 128), F32),
                pltpu.VMEM((8 + CHUNK, 128), F32),
                pltpu.VMEM((128, WIDTH_X), BF16),
                pltpu.VMEM((4, CHUNK, 128), F32),
                pltpu.VMEM((8, 128), F32),
                pltpu.VMEM((1, 256), F32),
                pltpu.VMEM((CHUNK, 128), F32),
                pltpu.VMEM((CHUNK, 128), F32),
                pltpu.VMEM((GROUP_W // 128, 8, 128), F32),
            ],
        ),
        out_shape=[
            jax.ShapeDtypeStruct((LOC, OWNERS, PAY, 128), BF16),
            jax.ShapeDtypeStruct((CHUNK, LOC * GROUP_W), BF16),
            jax.ShapeDtypeStruct((LOC, 2, CHUNK, 128), BF16),
            jax.ShapeDtypeStruct((LOC, 8, GROUP_W), F32),
        ],
        compiler_params=params(FIRST, "arbitrary"),
        cost_estimate=pl.CostEstimate(flops=2 * 10**9, bytes_accessed=18 * 10**6, transcendentals=0),
    )(ids, starts, xbc, recv, *rims, dt_raw, dt_recv, *tables)

    got = lax.all_to_all(pay.reshape(CHIPS, PAY, 128), ("y", "x", "z"), 0, 0, tiled=True)

    part = pl.pallas_call(
        inner_kernel,
        name="inner",
        grid=(LOC,),
        in_specs=[wide(GROUP_W), scale_spec, TABLE],
        out_specs=wide(WIDTH_X),
        out_shape=jax.ShapeDtypeStruct((CHUNK, LOC * WIDTH_X), F32),
        scratch_shapes=[pltpu.VMEM((128, WIDTH_X), BF16)],
        compiler_params=params(INNER, "arbitrary"),
        cost_estimate=pl.CostEstimate(flops=2 * 10**9, bytes_accessed=20 * 10**6, transcendentals=0),
    )(act, scale, tabs)

    held, fin = pl.pallas_call(
        scan_kernel,
        name="scan",
        in_specs=[SMEM, SMEM, SMEM, VMEM],
        out_specs=[VMEM, VMEM],
        out_shape=[
            jax.ShapeDtypeStruct((CHIPS, STATE, 128), BF16),
            jax.ShapeDtypeStruct((OWNERS, PAY, 128), BF16),
        ],
        scratch_shapes=[pltpu.VMEM((CHIPS, 128), F32), pltpu.VMEM((2 * OWNERS, STATE, 128), F32)],
        compiler_params=params(SCAN),
        cost_estimate=pl.CostEstimate(flops=10**7, bytes_accessed=5 * 10**6, transcendentals=0),
    )(ids, starts, assign, got)

    back = lax.all_to_all(held, ("y", "x", "z"), 0, 0, tiled=True)
    rows_got = lax.all_to_all(fin, ("x", "z"), 0, 0, tiled=True)

    back = back.reshape(LOC, OWNERS, STATE, 128)
    send = last_call(ids, part, act, scale, back, tabs, False)
    theirs = lax.ppermute(send, "core", swap)
    out = last_call(ids, part, act, scale, back, tabs, True)
    mixed = pl.pallas_call(
        place_kernel,
        name="place",
        in_specs=[SMEM, HBM, HBM],
        out_specs=HBM,
        out_shape=jax.ShapeDtypeStruct((ROWS, GROUPS * WIDTH_X), BF16),
        scratch_shapes=[
            pltpu.VMEM((LOC, ROWS, WIDTH_X), BF16),
            pltpu.SemaphoreType.DMA((LOC,)),
            pltpu.SemaphoreType.DMA((LOC,)),
        ],
        input_output_aliases={1: 0},
        compiler_params=params(PLACE),
    )(ids, out, theirs)
    states, tails = pl.pallas_call(
        rows_kernel,
        name="rows",
        in_specs=[VMEM],
        out_specs=[VMEM, VMEM],
        out_shape=[
            jax.ShapeDtypeStruct((OWNERS, STATE, 128), F32),
            jax.ShapeDtypeStruct((1, LAG, GROUP_W), BF16),
        ],
        compiler_params=params(EXTRA),
    )(rows_got)
    return (mixed, states.reshape(1, PER_GROUP, HEAD_DIM, STATE), tails)


def solution(mesh):
    axes = ("x", "z", "y", "core")
    fine = Mesh(mesh.devices.reshape(4, 4, 4, 2), axes)
    head = ("y", "core")
    in_specs = (
        P(axes, None),
        P(axes, None),
        P(head),
        P(head),
        P(None, head),
        P(head),
        P(head),
        P(),
        P(),
    )
    out_specs = (P(axes, None), P(("x", "z"), head, None, None), P(("x", "z"), None, head))
    return jax.shard_map(shards, mesh=fine, in_specs=in_specs, out_specs=out_specs, check_vma=False)
```

time: 152 us -> 146 us (0.961)
  Pallas kernels: 49.6 us -> 44 us
    pallas_call x1, Pallas kernels: 18 us -> 14.4 us  [shards(): pl.pallas_call(first_kernel, name='first', grid_spec=pltpu.PrefetchScalar...]
    pallas_call x6, Pallas kernels: 29.7 us -> 27.7 us  [the longest x2 10.9 us: last_call(): pl.pallas_call(functools.partial(last_kernel, row_at, col_at), name='last...]
  transfers between devices with their start and end apart: 9 -> 9, of which waited for: 4 -> 4; matrix products, arithmetic and copies ran while one was open for 0% -> 0% of each run, Pallas kernels for 12% -> 13%
where the time goes in v4:
time: 146 us; the launch traced here: 145 us
  blocking collectives  62.7 us (43%)
  Pallas kernels  44 us (30%)
  waiting for transfers between devices  22.1 us (15%)
  starting transfers between devices  13.5 us (9%)
  local copies, waits for them, and re-layouts  2.2 us (2%)
    all_to_all x1, blocking collectives, shards(): lax.all_to_all(pay.reshape(CHIPS, PAY, 128), ('y', 'x', 'z'), 0, 0, tiled...  46.9 us
    all_to_all x1, waiting for transfers between devices, shards(): back = lax.all_to_all(held, ('y', 'x', 'z'), 0, 0, tiled=True)  20.3 us
    all_to_all x1, blocking collectives, shards(): rows_got = lax.all_to_all(fin, ('x', 'z'), 0, 0, tiled=True)  15.8 us
    pallas_call x1, Pallas kernels, shards(): pl.pallas_call(first_kernel, name='first', grid_spec=pltpu.PrefetchScalar...  14.4 us
    pallas_call x2, Pallas kernels, last_call(): pl.pallas_call(functools.partial(last_kernel, row_at, col_at), name='last...  10.9 us
    pallas_call x1, Pallas kernels, shards(): pl.pallas_call(inner_kernel, name='inner', grid=(LOC,), in_specs=[wide(GR...  9.99 us
    ppermute x3, starting transfers between devices, shards(): lax.ppermute(table, 'y', [(i, (i + s) % 4) for i in range(4)])  5.94 us
    all_to_all x1, starting transfers between devices, shards(): back = lax.all_to_all(held, ('y', 'x', 'z'), 0, 0, tiled=True)  5.87 us
  transfers between devices with their start and end apart: 9, of which 4 were waited for; matrix products, arithmetic and copies ran while one was open for 0% of the time, Pallas kernels for 13%

profile of v4, /device:TPU:0, one launch (start us, length us, event | category | flops | bytes accessed | tf_op | source)
XLA Modules:
  0.0 145.4 jit_solution(16752943528555891329)
XLA Ops:
  0.6 0.0 copy-start.1
  0.6 0.0 copy-start.2
  0.7 0.1 collective-permute-start
  0.7 1.9 %table.1 = (f32[8,2304]{1,0:T(8,128)}, bf16[3,18432]{1,0:T(4,128)(2,1)}) custom-call(bf16[4,2304]{1,0:T(4,128)(2,1)} %conv_w.1, bf16[2304]{0:T(1024)(128)(2,1)} %conv_b.1, bf16[2048]{0:T(1024)(128)(2,1)} %gain.1, f32[32]{0:T(128)} %decay.1, f32[32]{0:T(128)} %skip.1, bf16[128,18432]{1,0:T(8,128)(2,1)} %mine.1), custom_call_target="tpu_custom_call" | custom-call | tf_op jit(solution)/shard_map/table/pallas_call | solution.py:361
  2.7 1.7 %collective-permute-start.4 = (f32[8,2304]{1,0:T(8,128)}, f32[8,2304]{1,0:T(8,128)S(1)}, u32[]{:S(2)}, u32[]{:S(2)}) collective-permute-start(f32[8,2304]{1,0:T(8,128)} %get-tuple-element.14.tab0), channel_id=1, source_target_pairs={{0,2},{2,4},{4,6},{6,0},{1,3},{3,5},{5,7},{7,1},{8,10},{10,12},{12... | collective-permute-start | bytes 221192 | tf_op jit(solution)/shard_map/ppermute | solution.py:386
  4.4 0.0 copy-done.1
  4.4 0.2 collective-permute-start.3
  4.6 2.9 %collective-permute-start.5 = (f32[8,2304]{1,0:T(8,128)}, f32[8,2304]{1,0:T(8,128)S(1)}, u32[]{:S(2)}, u32[]{:S(2)}) collective-permute-start(f32[8,2304]{1,0:T(8,128)} %get-tuple-element.14.tab0), channel_id=1, source_target_pairs={{0,4},{2,6},{4,0},{6,2},{1,5},{3,7},{5,1},{7,3},{8,12},{10,14},{12... | collective-permute-start | bytes 221192 | tf_op jit(solution)/shard_map/ppermute | solution.py:386
  7.5 1.3 collective-permute-start.6
  8.8 0.2 collective-permute-done.3.dt_recv
  9.0 0.7 collective-permute-start.1
  9.7 0.0 collective-permute-done.4.tab1
  9.7 0.7 collective-permute-start.2
  10.4 1.3 collective-permute-done.5.tab2
  11.7 0.3 collective-permute-done.6.tab3
  12.0 0.0 collective-permute-done.1.rim_a
  12.0 0.0 collective-permute-done.2.rim_b
  12.0 0.0 collective-permute-done.recv
  12.0 0.0 copy-done.2
  12.1 0.0 copy-start
  12.1 0.9 copy-done
  12.9 14.4 %first.1 = (bf16[4,16,136,128]{3,2,1,0:T(8,128)(2,1)}, bf16[256,9216]{1,0:T(8,128)(2,1)}, bf16[4,2,256,128]{3,2,1,0:T(8,128)(2,1)S(1)}, f32[4,8,2304]{2,1,0:T(8,128)S(1)}) custom-call(s32[4]{0:T(128)S(1)} %compare_select_fusion.1.ids, s32[16]{0:T(128)S(1)} %copy-done.2, bf16[128,18432]{1,0:T(8,128)(2,1)} %mine.1, ...), custom_call_target="tpu_custom_call" | custom-call | flops 2000000000 | bytes 18000000 | tf_op jit(solution)/shard_map/first/pallas_call | solution.py:395
  27.3 0.0 copy-start.3
  27.3 46.9 %all_to_all.15.got = bf16[64,136,128]{2,1,0:T(8,128)(2,1)S(1)} all-to-all(bf16[64,136,128]{2,1,0:T(8,128)(2,1)} %bitcast.5), channel_id=1, replica_groups=mesh['x'=4,'z'=4,'y'=4,'core'=2] {'y','x','z'}, dimensions={0} | all-to-all | bytes 4456448 | tf_op jit(solution)/shard_map/all_to_all | solution.py:431
  74.2 0.0 copy-done.3
  74.2 3.6 %scan.1 = (bf16[64,128,128]{2,1,0:T(8,128)(2,1)}, bf16[16,136,128]{2,1,0:T(8,128)(2,1)S(1)}) custom-call(s32[4]{0:T(128)S(1)} %compare_select_fusion.1.ids, s32[16]{0:T(128)S(1)} %copy-done.2, s32[4]{0:T(128)S(1)} %copy-done.3, bf16[64,136,128]{2,1,0:T(8,128)(2,1)S(1)} %all_to_all.15.got), custom_call_target="tpu_custom_call" | custom-call | flops 10000000 | bytes 5000000 | tf_op jit(solution)/shard_map/scan/pallas_call | solution.py:445
  77.8 5.9 %all-to-all-start.1 = ((bf16[64,128,128]{2,1,0:T(8,128)(2,1)}), bf16[64,128,128]{2,1,0:T(8,128)(2,1)S(1)}, u32[]{:S(2)}, u32[]{:S(2)}) async-start(bf16[64,128,128]{2,1,0:T(8,128)(2,1)} %get-tuple-element.19), calls=%async_computation.1 | async-start | bytes 4194304 | tf_op jit(solution)/shard_map/all_to_all | solution.py:459
  83.7 10.0 %inner.1.part = f32[256,8192]{1,0:T(8,128)} custom-call(bf16[256,9216]{1,0:T(8,128)(2,1)} %get-tuple-element.15.act, bf16[4,2,256,128]{3,2,1,0:T(8,128)(2,1)S(1)} %get-tuple-element.16.scale, f32[4,8,2304]{2,1,0:T(8,128)S(1)} %get-tuple-element.17.tabs), custom_call_target="tpu_custom_call" | custom-call | flops 2000000000 | bytes 20000000 | tf_op jit(solution)/shard_map/inner/pallas_call | solution.py:433
  93.7 20.3 %all-to-all-done.1 = bf16[64,128,128]{2,1,0:T(8,128)(2,1)S(1)} async-done(((bf16[64,128,128]{2,1,0:T(8,128)(2,1)}), bf16[64,128,128]{2,1,0:T(8,128)(2,1)S(1)}, u32[]{:S(2)}, u32[]{:S(2)}) %all-to-all-start.1) | async-done | bytes 2097184 | tf_op jit(solution)/shard_map/all_to_all | solution.py:459
  113.9 0.0 copy-start.4
  113.9 1.3 copy-done.4
  115.2 5.5 %last.3 = bf16[128,8192]{1,0:T(8,128)(2,1)} custom-call(s32[4]{0:T(128)S(1)} %compare_select_fusion.1.ids, f32[256,8192]{1,0:T(8,128)} %inner.1.part, bf16[256,9216]{1,0:T(8,128)(2,1)} %get-tuple-element.15.act, bf16[4,2,256,128]{3,2,1,0:T(8,128)(2,1)S(1)} %get-tuple-element.16.scale, bf16[4,16,128,128]{3,2,1,0:T(8,128)(2,1)} %bitcast.3, ...), custom_call_target="tpu_custom_call" | custom-call | flops 1000000000 | bytes 9000000 | tf_op jit(solution)/shard_map/last/pallas_call | solution.py:326
  120.8 0.1 collective-permute-start.7
  120.8 15.8 %all_to_all.16.got = bf16[16,136,128]{2,1,0:T(8,128)(2,1)S(1)} all-to-all(bf16[16,136,128]{2,1,0:T(8,128)(2,1)S(1)} %get-tuple-element.20), channel_id=1, replica_groups=mesh['x'=4,'z'=4,'y'=4,'core'=2] {'x','z'}, dimensions={0} | all-to-all | bytes 1114112 | tf_op jit(solution)/shard_map/all_to_all | solution.py:460
  136.7 1.1 rows.3
  137.8 5.4 %last.2.whole = bf16[128,16384]{1,0:T(8,128)(2,1)} custom-call(s32[4]{0:T(128)S(1)} %compare_select_fusion.1.ids, f32[256,8192]{1,0:T(8,128)} %inner.1.part, bf16[256,9216]{1,0:T(8,128)(2,1)} %get-tuple-element.15.act, bf16[4,2,256,128]{3,2,1,0:T(8,128)(2,1)S(1)} %get-tuple-element.16.scale, bf16[4,16,128,128]{3,2,1,0:T(8,128)(2,1)} %bitcast.4, ...), custom_call_target="tpu_custom_call" | custom-call | flops 1000000000 | bytes 9000000 | tf_op jit(solution)/shard_map/last/pallas_call | solution.py:326
  143.2 0.0 collective-permute-done.7.theirs
  143.2 2.1 %place.1 = bf16[128,16384]{1,0:T(8,128)(2,1)} custom-call(s32[4]{0:T(128)S(1)} %compare_select_fusion.1.ids, bf16[128,16384]{1,0:T(8,128)(2,1)} %last.2.whole, bf16[128,8192]{1,0:T(8,128)(2,1)S(1)} %collective-permute-done.7.theirs), custom_call_target="tpu_custom_call", output_to_operand_aliasing={{}: (1, {})} | custom-call | tf_op jit(solution)/shard_map/place/pallas_call | solution.py:466
  (1 shorter events, 0.0 us)
Async XLA Ops:
  0.6 3.7 %copy-start.1 = (bf16[128,256]{1,0:T(8,128)(2,1)S(1)}, bf16[128,256]{1,0:T(8,128)(2,1)}, u32[]{:S(2)}) copy-start(bf16[128,256]{1,0:T(8,128)(2,1)} %dt_mine.1) | copy-start | bytes 196612
  0.6 11.4 %copy-start.2 = (s32[16]{0:T(128)S(1)}, s32[16]{0:T(128)}, u32[]{:S(2)}) copy-start(s32[16]{0:T(128)} %starts.3) | copy-start | bytes 196
  0.7 11.4 %collective-permute-start = (bf16[128,18432]{1,0:T(8,128)(2,1)}, bf16[128,18432]{1,0:T(8,128)(2,1)}, u32[]{:S(2)}, u32[]{:S(2)}) collective-permute-start(bf16[128,18432]{1,0:T(8,128)(2,1)} %mine.1), channel_id=1, source_target_pairs={{0,1},{1,0},{2,3},{3,2},{4,5},{5,4},{6,7},{7,6},{8,9},{9,8},{10,11... | collective-permute-start | bytes 14155784 | tf_op jit(solution)/shard_map/ppermute | solution.py:357
  2.7 7.0 %collective-permute-start.4 = (f32[8,2304]{1,0:T(8,128)}, f32[8,2304]{1,0:T(8,128)S(1)}, u32[]{:S(2)}, u32[]{:S(2)}) collective-permute-start(f32[8,2304]{1,0:T(8,128)} %get-tuple-element.14.tab0), channel_id=1, source_target_pairs={{0,2},{2,4},{4,6},{6,0},{1,3},{3,5},{5,7},{7,1},{8,10},{10,12},{12... | collective-permute-start | bytes 221192 | tf_op jit(solution)/shard_map/ppermute | solution.py:386
  4.4 4.6 %collective-permute-start.3 = (bf16[128,256]{1,0:T(8,128)(2,1)S(1)}, bf16[128,256]{1,0:T(8,128)(2,1)S(1)}, u32[]{:S(2)}, u32[]{:S(2)}) collective-permute-start(bf16[128,256]{1,0:T(8,128)(2,1)S(1)} %copy-done.1), channel_id=1, source_target_pairs={{0,1},{1,0},{2,3},{3,2},{4,5},{5,4},{6,7},{7,6},{8,9},{9,8},{10,11... | collective-permute-start | bytes 196616 | tf_op jit(solution)/shard_map/ppermute | solution.py:358
  4.6 7.1 %collective-permute-start.5 = (f32[8,2304]{1,0:T(8,128)}, f32[8,2304]{1,0:T(8,128)S(1)}, u32[]{:S(2)}, u32[]{:S(2)}) collective-permute-start(f32[8,2304]{1,0:T(8,128)} %get-tuple-element.14.tab0), channel_id=1, source_target_pairs={{0,4},{2,6},{4,0},{6,2},{1,5},{3,7},{5,1},{7,3},{8,12},{10,14},{12... | collective-permute-start | bytes 221192 | tf_op jit(solution)/shard_map/ppermute | solution.py:386
  7.5 4.6 %collective-permute-start.6 = (f32[8,2304]{1,0:T(8,128)}, f32[8,2304]{1,0:T(8,128)S(1)}, u32[]{:S(2)}, u32[]{:S(2)}) collective-permute-start(f32[8,2304]{1,0:T(8,128)} %get-tuple-element.14.tab0), channel_id=1, source_target_pairs={{0,6},{2,0},{4,2},{6,4},{1,7},{3,1},{5,3},{7,5},{8,14},{10,8},{12,... | collective-permute-start | bytes 221192 | tf_op jit(solution)/shard_map/ppermute | solution.py:386
  9.0 3.0 %collective-permute-start.1 = (bf16[3,18432]{1,0:T(4,128)(2,1)}, bf16[3,18432]{1,0:T(4,128)(2,1)S(1)}, u32[]{:S(2)}, u32[]{:S(2)}) collective-permute-start(bf16[3,18432]{1,0:T(4,128)(2,1)} %get-tuple-element.13), channel_id=1, source_target_pairs={{1,2},{3,4},{5,6},{7,8},{9,10},{11,12},{13,14},{15,16},{17,18},{19... | collective-permute-start | bytes 331784 | tf_op jit(solution)/shard_map/ppermute | solution.py:382
  9.7 2.4 %collective-permute-start.2 = (bf16[3,18432]{1,0:T(4,128)(2,1)}, bf16[3,18432]{1,0:T(4,128)(2,1)S(1)}, u32[]{:S(2)}, u32[]{:S(2)}) collective-permute-start(bf16[3,18432]{1,0:T(4,128)(2,1)} %get-tuple-element.13), channel_id=1, source_target_pairs={{1,3},{3,5},{5,7},{7,9},{9,11},{11,13},{13,15},{15,17},{17,19},{19... | collective-permute-start | bytes 331784 | tf_op jit(solution)/shard_map/ppermute | solution.py:382
  12.1 0.9 copy-start
  27.3 46.9 %copy-start.3 = (s32[4]{0:T(128)S(1)}, s32[4]{0:T(128)}, u32[]{:S(2)}) copy-start(s32[4]{0:T(128)} %assign.1) | copy-start | bytes 52
  77.8 36.1 %all-to-all-start.1 = ((bf16[64,128,128]{2,1,0:T(8,128)(2,1)}), bf16[64,128,128]{2,1,0:T(8,128)(2,1)S(1)}, u32[]{:S(2)}, u32[]{:S(2)}) async-start(bf16[64,128,128]{2,1,0:T(8,128)(2,1)} %get-tuple-element.19), calls=%async_computation.1 | async-start | bytes 4194304 | tf_op jit(solution)/shard_map/all_to_all | solution.py:459
  113.9 1.3 copy-start.4
  120.8 22.5 %collective-permute-start.7 = (bf16[128,8192]{1,0:T(8,128)(2,1)}, bf16[128,8192]{1,0:T(8,128)(2,1)S(1)}, u32[]{:S(2)}, u32[]{:S(2)}) collective-permute-start(bf16[128,8192]{1,0:T(8,128)(2,1)} %last.3), channel_id=1, source_target_pairs={{0,1},{1,0},{2,3},{3,2},{4,5},{5,4},{6,7},{7,6},{8,9},{9,8},{10,11... | collective-permute-start | bytes 6291464 | tf_op jit(solution)/shard_map/ppermute | solution.py:464
